TPU v7x, 128 devices: a whole 4x4x4 slice. The times are simulated.
128 devices in a mesh: row: 16 (over x, z), col: 8 (over y, core).
Axes of the slice: x: 4, y: 4, z: 4, core: 2. Of those that a mesh axis runs over, the one named last changes fastest.
Arguments:
- teacher_rows: bfloat16 [256, 8192], P('col', 'row'), may hold values from -6 to 6
- projection: bfloat16 [8192, 4608], P('row'), may hold values from -0.0625 to 0.0625
- student_in: bfloat16 [256, 4608], P('col', 'row'), may hold values from -36 to 36, as said below
- norm_gain: bfloat16 [4608], P('row'), may hold values from 0.5 to 1.5
- w_gate: bfloat16 [4608, 36864], P('row', 'col'), may hold values from -0.09375 to 0.09375
- w_up: bfloat16 [4608, 36864], P('row', 'col'), may hold values from -0.09375 to 0.09375
- w_down: bfloat16 [4608, 36864], P('row', 'col'), may hold values from -0.03125 to 0.03125
- row_old: float32 [3, 4608], P(None, 'row'), may hold values from 1.953125e-05 to 0.001953125
- col_old: float32 [3, 36864], P(None, 'col'), may hold values from 1.953125e-05 to 0.001953125
Outputs:
- update_gate: bfloat16 [4608, 36864], P('row', 'col')
- update_up: bfloat16 [4608, 36864], P('row', 'col')
- update_down: bfloat16 [4608, 36864], P('row', 'col')
- row_factors: float32 [3, 4608], P(None, 'row')
- col_factors: float32 [3, 36864], P(None, 'col')
- distill_loss: float32 [], replicated
Inputs may be any that keep to these rules, and one draw needn't show every extreme that they name: `student_in`: student hidden rows of varying magnitude.
All inputs are finite; a program needn't handle non-finite values.
Results may differ from a plain program's by a relative error of at most 0.0075.
Values may be sent and summed in bfloat16 or wider, within the bound.
A program may use at most 128 MiB of HBM per device.

v0:
```python
import math

import jax
import jax.numpy as jnp
from jax import lax
from jax.sharding import PartitionSpec as P

D = 4608
FF = 36864


def gelu_pair(values):
    root_coef = math.sqrt(2.0 / math.pi)
    tangent = jnp.tanh(root_coef * (values + 0.044715 * values * values * values))
    gelu_val = 0.5 * values * (1.0 + tangent)
    gelu_slope = 0.5 * (1.0 + tangent) + 0.5 * values * (1.0 - tangent * tangent) * root_coef * (
        1.0 + 3.0 * 0.044715 * values * values
    )
    return (gelu_val, gelu_slope)


def shards(teacher_rows, projection, student_in, norm_gain, w_gate, w_up, w_down, row_old, col_old):
    decay_rate = 0.8
    target = lax.psum_scatter(
        lax.dot_general(
            projection, teacher_rows, (((0,), (1,)), ((), ())), preferred_element_type=jnp.float32
        ),
        "row",
        scatter_dimension=0,
        tiled=True,
    ).T.astype(jnp.bfloat16)
    inputs = student_in.astype(jnp.float32)
    mean_sq = lax.psum(jnp.sum(inputs * inputs, axis=1), "row") / D
    inv_rms = (1.0 / jnp.sqrt(mean_sq + 1e-06))[:, None]
    normed = (inputs * inv_rms * norm_gain.astype(jnp.float32)[None, :]).astype(jnp.bfloat16)
    normed_all = lax.all_gather(normed, "col", axis=0, tiled=True)
    tokens_all = normed_all.shape[0]
    gate_part = jnp.dot(normed_all, w_gate, preferred_element_type=jnp.float32)
    up_part = jnp.dot(normed_all, w_up, preferred_element_type=jnp.float32)
    gate_sum, up_sum = lax.psum((gate_part, up_part), "row")
    gelu_val, gelu_slope = gelu_pair(gate_sum)
    hidden = (gelu_val * up_sum).astype(jnp.bfloat16)
    down_out = lax.psum_scatter(
        lax.dot_general(
            hidden, w_down, (((1,), (1,)), ((), ())), preferred_element_type=jnp.float32
        ),
        "col",
        scatter_dimension=0,
        tiled=True,
    )
    residue = inputs + down_out - target.astype(jnp.float32)
    loss_local = jnp.sum(residue * residue)
    loss_raw = lax.psum(loss_local, ("row", "col"))
    grad_out = (residue / tokens_all).astype(jnp.bfloat16)
    grad_all = lax.all_gather(grad_out, "col", axis=0, tiled=True)
    grad_down = lax.dot_general(
        grad_all, hidden, (((0,), (0,)), ((), ())), preferred_element_type=jnp.float32
    )
    hidden_part = jnp.dot(grad_all, w_down, preferred_element_type=jnp.float32)
    grad_hidden = lax.psum(hidden_part, "row")
    grad_gatein = (grad_hidden * up_sum * gelu_slope).astype(jnp.bfloat16)
    grad_upin = (grad_hidden * gelu_val).astype(jnp.bfloat16)
    grad_gate = lax.dot_general(
        normed_all, grad_gatein, (((0,), (0,)), ((), ())), preferred_element_type=jnp.float32
    )
    grad_up = lax.dot_general(
        normed_all, grad_upin, (((0,), (0,)), ((), ())), preferred_element_type=jnp.float32
    )
    gradients = [grad_gate, grad_up, grad_down]
    squares = [gradient * gradient + 1e-30 for gradient in gradients]
    row_sums = lax.psum(
        (jnp.sum(squares[0], axis=1), jnp.sum(squares[1], axis=1), jnp.sum(squares[2], axis=1)),
        "col",
    )
    col_sums = lax.psum(
        (jnp.sum(squares[0], axis=0), jnp.sum(squares[1], axis=0), jnp.sum(squares[2], axis=0)),
        "row",
    )
    row_new = [
        decay_rate * row_old[which] + (1.0 - decay_rate) * row_sums[which] / FF
        for which in range(3)
    ]
    col_new = [
        decay_rate * col_old[which] + (1.0 - decay_rate) * col_sums[which] / D for which in range(3)
    ]
    updates = [
        gradients[which] / jnp.sqrt(row_new[which][:, None] * col_new[which][None, :])
        for which in range(3)
    ]
    update_sums = [jnp.sum(update * update) for update in updates]
    totals = lax.psum((update_sums[0], update_sums[1], update_sums[2]), ("row", "col"))
    clipped = [
        (updates[which] / jnp.maximum(1.0, jnp.sqrt(totals[which] / (D * FF)))).astype(jnp.bfloat16)
        for which in range(3)
    ]
    loss_total = 0.5 * loss_raw / tokens_all
    return (clipped[0], clipped[1], clipped[2], jnp.stack(row_new), jnp.stack(col_new), loss_total)


def solution(mesh):
    placed = (
        P("col", "row"),
        P("row", None),
        P("col", "row"),
        P("row"),
        P("row", "col"),
        P("row", "col"),
        P("row", "col"),
        P(None, "row"),
        P(None, "col"),
    )
    return jax.shard_map(
        shards,
        mesh=mesh,
        in_specs=placed,
        out_specs=(
            P("row", "col"),
            P("row", "col"),
            P("row", "col"),
            P(None, "row"),
            P(None, "col"),
            P(),
        ),
        check_vma=False,
    )
```

profile of v0, /device:TPU:1, one launch (start us, length us, event | category | flops | bytes accessed | tf_op | source)
XLA Modules:
  0.0 661.3 jit_solution(16342523229148362279)
XLA Ops:
  8.9 35.4 %psum.98 = f32[32]{0:T(128)S(1)} all-reduce(f32[32]{0:T(128)S(1)} %fusion.16), channel_id=1, replica_groups=mesh['row'=16,'col'=8] {'row'}, use_global_device_ids=true, to_apply=%region_1.0 | all-reduce | flops 32 | bytes 256 | tf_op jit(solution)/shard_map/psum | solution.py:33
  45.3 20.9 %all_gather.6 = bf16[256,288]{1,0:T(8,128)(2,1)S(1)} all-gather(bf16[32,288]{1,0:T(8,128)(2,1)S(1)} %fusion.18), channel_id=1, replica_groups=mesh['row'=16,'col'=8] {'col'}, dimensions={0}, use_global_device_ids=true | all-gather | bytes 165888 | tf_op jit(solution)/shard_map/all_gather | solution.py:36
  66.2 5.3 fusion.29
  71.5 3.6 fusion.30
  75.8 5.7 fusion.33
  81.6 138.9 %all-reduce.9.cloned.1.call-done = (f32[256,4608]{1,0:T(8,128)}, f32[256,4608]{1,0:T(8,128)}) async-done(((f32[256,4608]{1,0:T(8,128)}, f32[256,4608]{1,0:T(8,128)}), (f32[256,4608]{1,0:T(8,128)}, f32[256,4608]{1,0:T(8,128)})) %all-reduce.9.cloned.1.call-update) | async-done | bytes 9437200 | tf_op jit(solution)/shard_map/psum | solution.py:40
  220.5 4.6 multiply_convert_fusion.1
  228.7 69.7 %reduce-scatter.7.cloned.1.call-done = f32[288,32]{1,0:T(8,128)} async-done(((f32[4608,32]{1,0:T(8,128)}), f32[288,32]{1,0:T(8,128)}) %reduce-scatter.7.cloned.1.call-update) | async-done | bytes 36880
  299.4 31.4 %reduce-scatter.5.cloned.1.call-done = f32[32,288]{1,0:T(8,128)} async-done(((f32[256,288]{1,0:T(8,128)}), f32[32,288]{1,0:T(8,128)}) %reduce-scatter.5.cloned.1.call-update) | async-done | bytes 36880 | tf_op jit(solution)/shard_map/reduce_scatter | solution.py:43
  332.3 16.1 %all_gather.7 = bf16[256,288]{1,0:T(8,128)(2,1)S(1)} all-gather(bf16[32,288]{1,0:T(8,128)(2,1)S(1)} %get-tuple-element.31), channel_id=1, replica_groups=mesh['row'=16,'col'=8] {'col'}, dimensions={0}, use_global_device_ids=true | all-gather | bytes 165888 | tf_op jit(solution)/shard_map/all_gather | solution.py:55
  348.3 3.6 fusion.32
  353.6 3.3 fusion.12
  356.9 102.5 %all-reduce.7.cloned.1.call-done = f32[256,4608]{1,0:T(8,128)} async-done(((f32[256,4608]{1,0:T(8,128)}), f32[256,4608]{1,0:T(8,128)}) %all-reduce.7.cloned.1.call-update) | async-done | bytes 4718608 | tf_op jit(solution)/shard_map/psum | solution.py:60
  459.3 9.0 %fusion.8 = (f32[288]{0:T(512)S(1)}, f32[4608]{0:T(1024)S(1)}, f32[288,4608]{1,0:T(8,128)}) fusion(bf16[256,288]{1,0:T(8,128)(2,1)S(1)} %all_gather.6, f32[256,4608]{1,0:T(8,128)} %get-tuple-element.25, f32[256,4608]{1,0:T(8,128)} %all-reduce.7.cloned.1.call-done, f32[256,4608]{1,0:T(8,128)} %get-tuple-element.26), kind=kOutput, calls=%fused_computation.24 | convolution fusion | flops 708373760 | bytes 19631232 | tf_op jit(solution)/shard_map/dot_general | solution.py:63
  468.3 7.3 %fusion.10 = (f32[288]{0:T(512)S(1)}, f32[4608]{0:T(1024)S(1)}, f32[288,4608]{1,0:T(8,128)}) fusion(bf16[256,288]{1,0:T(8,128)(2,1)S(1)} %all_gather.6, f32[256,4608]{1,0:T(8,128)S(1)} %copy-done.11, f32[256,4608]{1,0:T(8,128)} %get-tuple-element.25), kind=kOutput, calls=%fused_computation.26 | convolution fusion | flops 696577280 | bytes 14912640 | tf_op jit(solution)/shard_map/dot_general | solution.py:66
  475.7 12.8 %all-reduce.3 = (f32[288]{0:T(512)S(1)}, f32[288]{0:T(512)S(1)}, f32[288]{0:T(512)S(1)}) all-reduce(f32[288]{0:T(512)S(1)} %get-tuple-element.10, f32[288]{0:T(512)S(1)} %get-tuple-element.8, f32[288]{0:T(512)S(1)} %get-tuple-element.6), channel_id=1, replica_groups=mesh['row'=16,'col'=8] {'col'}, use_global_device_ids=true, to_apply=%region_8.0 | all-reduce | flops 864 | bytes 6912 | tf_op jit(solution)/shard_map/psum | solution.py:71
  488.5 58.5 %all-reduce.1 = (f32[4608]{0:T(1024)S(1)}, f32[4608]{0:T(1024)S(1)}, f32[4608]{0:T(1024)S(1)}) all-reduce(f32[4608]{0:T(1024)S(1)} %get-tuple-element.11, f32[4608]{0:T(1024)S(1)} %get-tuple-element.9, f32[4608]{0:T(1024)S(1)} %get-tuple-element.7), channel_id=1, replica_groups=mesh['row'=16,'col'=8] {'row'}, use_global_device_ids=true, to_apply=%region_10.0 | all-reduce | flops 13824 | bytes 110592 | tf_op jit(solution)/shard_map/psum | solution.py:75
  547.0 4.7 multiply_reduce_fusion.2
  551.7 2.4 multiply_reduce_fusion.1
  554.1 2.4 multiply_reduce_fusion
  556.5 78.3 %all-reduce = (f32[]{:T(128)}, f32[]{:T(128)}, f32[]{:T(128)}, f32[]{:T(128)}) all-reduce(f32[]{:T(128)} %multiply_reduce_fusion.2, f32[]{:T(128)} %multiply_reduce_fusion.1, f32[]{:T(128)} %multiply_reduce_fusion, f32[]{:T(128)} %get-tuple-element.30), channel_id=1, replica_groups=mesh['row'=16,'col'=8] {'row','col'}, use_global_device_ids=true, to_apply=%region_12.0 | all-reduce | flops 4 | bytes 32 | tf_op jit(solution)/shard_map/psum | solution.py:91
  635.5 4.9 divide_convert_fusion.2
  641.1 5.0 divide_convert_fusion.1
  646.8 4.9 divide_convert_fusion
  (53 shorter events, 12.5 us)
Async XLA Ops:
  7.2 219.3 %copy-start = (bf16[288,4608]{1,0:T(8,128)(2,1)S(1)}, bf16[288,4608]{1,0:T(8,128)(2,1)}, u32[]{:S(2)}) copy-start(bf16[288,4608]{1,0:T(8,128)(2,1)} %param.15) | copy-start | bytes 7962628
  7.2 213.3 %all-reduce.9.cloned.1.call-start = ((), (), s32[]{:S(2)}) async-start(), calls=%async_computation.5 | async-start | bytes 18874368 | tf_op jit(solution)/shard_map/psum | solution.py:40
  44.3 27.2 %copy-start.6 = (bf16[288,4608]{1,0:T(8,128)(2,1)S(1)}, bf16[288,4608]{1,0:T(8,128)(2,1)}, u32[]{:S(2)}) copy-start(bf16[288,4608]{1,0:T(8,128)(2,1)} %param.14) | copy-start | bytes 7962628
  75.0 0.8 copy-start.9
  75.1 223.4 %reduce-scatter.7.cloned.1.call-start = ((), (), s32[]{:S(2)}) async-start(), calls=%async_computation.4 | async-start | bytes 2506752
  81.5 249.3 %reduce-scatter.5.cloned.1.call-start = ((), (), s32[]{:S(2)}) async-start(), calls=%async_computation.2 | async-start | bytes 442368 | tf_op jit(solution)/shard_map/reduce_scatter | solution.py:43
  225.1 1.4 copy-start.4
  226.5 104.3 %copy-start.7 = (bf16[32,288]{1,0:T(8,128)(2,1)S(1)}, bf16[32,288]{1,0:T(8,128)(2,1)}, u32[]{:S(2)}) copy-start(bf16[32,288]{1,0:T(8,128)(2,1)} %param.11) | copy-start | bytes 55300
  228.7 230.7 %all-reduce.7.cloned.1.call-start = ((), (), s32[]{:S(2)}) async-start(), calls=%async_computation.3 | async-start | bytes 9437184 | tf_op jit(solution)/shard_map/psum | solution.py:60
  348.3 3.6 copy-start.10
  348.3 3.6 copy-start.8
  351.9 1.7 copy-start.5
  459.3 9.0 %copy-start.11 = (f32[256,4608]{1,0:T(8,128)S(1)}, f32[256,4608]{1,0:T(8,128)}, u32[]{:S(2)}) copy-start(f32[256,4608]{1,0:T(8,128)} %all-reduce.7.cloned.1.call-done) | copy-start | bytes 14155780
  546.9 4.8 copy-start.3
  547.0 7.2 %copy-start.2 = (f32[288,4608]{1,0:T(8,128)S(1)}, f32[288,4608]{1,0:T(8,128)}, u32[]{:S(2)}) copy-start(f32[288,4608]{1,0:T(8,128)} %get-tuple-element.34) | copy-start | bytes 15925252
  641.1 12.6 %copy-start.1 = (bf16[288,4608]{1,0:T(8,128)(2,1)S(1)}, bf16[288,4608]{1,0:T(8,128)(2,1)}, u32[]{:S(2)}) copy-start(bf16[288,4608]{1,0:T(8,128)(2,1)} %param.15) | copy-start | bytes 7962628
Sparse Core Ops, SparseCore 0:
  75.2 145.2 all-reduce.8
  224.4 74.0 reduce-scatter.6
  301.4 29.4 reduce-scatter.4
  352.1 107.2 all-reduce.6
where the time goes:
time: 662 us; the launch traced here: 661 us
  waiting for transfers between devices  343 us (52%)
  blocking collectives  222 us (34%)
  matrix products  39.8 us (6%)
  other arithmetic  34.5 us (5%)
  between operations  17.8 us (3%)
    psum x1, waiting for transfers between devices, shards(): gate_sum, up_sum = lax.psum((gate_part, up_part), 'row')  139 us
    psum x1, waiting for transfers between devices, shards(): grad_hidden = lax.psum(hidden_part, 'row')  102 us
    psum x1, blocking collectives, shards(): lax.psum((update_sums[0], update_sums[1], update_sums[2]), ('row', 'col'))  78.3 us
    unnamed x5, waiting for transfers between devices  69.8 us
    psum x1, blocking collectives, shards(): lax.psum((jnp.sum(squares[0], axis=0), jnp.sum(squares[1], axis=0), jnp.s...  58.5 us
    psum x1, blocking collectives, shards(): mean_sq = lax.psum(jnp.sum(inputs * inputs, axis=1), 'row') / D  35.4 us
    reduce_scatter x1, waiting for transfers between devices, shards(): lax.psum_scatter(lax.dot_general(hidden, w_down, (((1,), (1,)), ((), ()))...  31.4 us
    all_gather x1, blocking collectives, shards(): normed_all = lax.all_gather(normed, 'col', axis=0, tiled=True)  20.9 us
  transfers between devices with their start and end apart: 4, of which 4 were waited for; matrix products, arithmetic and copies ran while one was open for 3% of the time, Pallas kernels for 0%

commit v1 on v0

v1 whole, which is shorter than its diff:
```python
import math

import jax
import jax.numpy as jnp
from jax import lax
from jax.experimental import pallas as pl
from jax.experimental.pallas import tpu as pltpu
from jax.sharding import PartitionSpec as P

D = 4608
FF = 36864
TOKENS = 256
NR = 16
NC = 8
DL = D // NR
FL = FF // NC
FH = FL // 2
TL = TOKENS // NC
TILE = 768
F32 = jnp.float32
BF16 = jnp.bfloat16
VMEM_LIMIT = 62 * 1024 * 1024


def gelu_pair(values):
    root_coef = math.sqrt(2.0 / math.pi)
    tangent = jnp.tanh(root_coef * (values + 0.044715 * values * values * values))
    gelu_val = 0.5 * values * (1.0 + tangent)
    gelu_slope = 0.5 * (1.0 + tangent) + 0.5 * values * (1.0 - tangent * tangent) * root_coef * (
        1.0 + 3.0 * 0.044715 * values * values
    )
    return (gelu_val, gelu_slope)


def remote(src, dst, send_sem, recv_sem, axis, index):
    return pltpu.make_async_remote_copy(
        src_ref=src,
        dst_ref=dst,
        send_sem=send_sem,
        recv_sem=recv_sem,
        device_id={axis: index},
        device_id_type=pl.DeviceIdType.MESH,
    )


def enter(me, c):
    barrier = pltpu.get_barrier_semaphore()
    for d in range(1, NR):
        pl.semaphore_signal(
            barrier, inc=1, device_id={"row": lax.rem(me + d, NR)},
            device_id_type=pl.DeviceIdType.MESH,
        )
    for d in range(1, NC):
        pl.semaphore_signal(
            barrier, inc=1, device_id={"col": lax.rem(c + d, NC)},
            device_id_type=pl.DeviceIdType.MESH,
        )
    pl.semaphore_wait(barrier, NR + NC - 2)


def exchange(axis, me, n, source, slots, send_sem, recv_sem):
    copies = []
    for d in range(1, n):
        peer = lax.rem(me + d, n)
        copy = remote(
            source(peer), slots(d), send_sem.at[d - 1], recv_sem.at[d - 1], axis, peer
        )
        copy.start()
        copies.append(copy)
    return copies


def finish(copies):
    for copy in copies:
        copy.wait_recv()
    for copy in copies:
        copy.wait_send()


class Scatter:
    def __init__(self, buf, rows, lo, width, p, plus, minus, recv, acc, ss, rs):
        self.buf, self.rows, self.lo, self.half = buf, rows, lo, width // 2
        self.p, self.plus, self.minus = p, plus, minus
        self.recv, self.acc, self.ss, self.rs = recv, acc, ss, rs

    def part(self, k, which):
        at = pl.multiple_of(lax.rem(self.p + k, 4) * self.rows, 16)
        return self.buf.at[pl.ds(at, self.rows), pl.ds(self.lo + which * self.half, self.half)]

    def send(self, src, slot, to):
        copy = remote(
            src, self.recv.at[slot], self.ss.at[slot], self.rs.at[slot], "row", to
        )
        copy.start()
        return copy

    def start(self):
        self.copies = [
            self.send(self.part(2, 0), 0, self.plus),
            self.send(self.part(2, 1), 1, self.minus),
            self.send(self.part(1, 1), 2, self.plus),
            self.send(self.part(3, 0), 3, self.minus),
        ]

    def relay(self):
        self.copies[0].wait_recv()
        self.acc[0] = (self.part(1, 0)[...].astype(F32) + self.recv[0].astype(F32)).astype(BF16)
        self.copies.append(self.send(self.acc.at[0], 4, self.plus))
        self.copies[1].wait_recv()
        self.acc[1] = (self.part(3, 1)[...].astype(F32) + self.recv[1].astype(F32)).astype(BF16)
        self.copies.append(self.send(self.acc.at[1], 5, self.minus))

    def result(self):
        for at in (3, 2, 4, 5):
            self.copies[at].wait_recv()
        first = self.part(0, 0)[...].astype(F32) + self.recv[3].astype(F32) + self.recv[4].astype(F32)
        second = self.part(0, 1)[...].astype(F32) + self.recv[2].astype(F32) + self.recv[5].astype(F32)
        return (first, second)

    def drain(self):
        for copy in self.copies:
            copy.wait_send()


class Gather:
    def __init__(self, buf, base, rows, lo, width, p, plus, minus, ss, rs):
        self.buf, self.base, self.rows, self.lo, self.width = buf, base, rows, lo, width
        self.p, self.plus, self.minus, self.ss, self.rs = p, plus, minus, ss, rs

    def part(self, k, lo, width):
        at = pl.multiple_of(self.base + lax.rem(self.p + k, 4) * self.rows, 16)
        return self.buf.at[pl.ds(at, self.rows), pl.ds(self.lo + lo, width)]

    def send(self, ref, slot, to):
        copy = remote(ref, ref, self.ss.at[slot], self.rs.at[slot], "row", to)
        copy.start()
        return copy

    def start(self):
        self.copies = [
            self.send(self.part(0, 0, self.width), 0, self.plus),
            self.send(self.part(0, 0, self.width), 1, self.minus),
        ]

    def relay(self):
        half = self.width // 2
        self.copies[0].wait_recv()
        self.copies.append(self.send(self.part(3, 0, half), 2, self.plus))
        self.copies[1].wait_recv()
        self.copies.append(self.send(self.part(1, half, half), 3, self.minus))

    def done(self):
        self.copies[2].wait_recv()
        self.copies[3].wait_recv()

    def drain(self):
        for copy in self.copies:
            copy.wait_send()


def eye(rows, lanes):
    return lax.broadcasted_iota(jnp.int32, (rows, lanes), 0) == lax.broadcasted_iota(
        jnp.int32, (rows, lanes), 1
    )


def step_kernel(
    teacher, projection, student, gain, w_gate, w_up, w_down,
    normed_out, dy_out, hidden_out, grads_out, loss_out,
    proj_v, wg_v, wu_v, wd_v, sq, sq_in, tpart, tpart_in, normed, part, mid, recv1, acc1,
    recv2, acc2, hidden, act_v, ups_v, down_acc, down_part, down_in, dy, gpart, gmid,
    grecv1, gacc1, grecv2, gacc2, grads,
    load_sem, out_sem, sq_ss, sq_rs, t_ss, t_rs, n_ss, n_rs, d_ss, d_rs, y_ss, y_rs,
    s_ss, s_rs, g_ss, g_rs,
):
    me = lax.axis_index("row")
    c = lax.axis_index("col")
    x, z = lax.div(me, 4), lax.rem(me, 4)
    loads = [
        pltpu.make_async_copy(src, dst, load_sem.at[i])
        for i, (src, dst) in enumerate(
            ((projection, proj_v), (w_gate, wg_v), (w_up, wu_v), (w_down, wd_v))
        )
    ]
    for load in loads:
        load.start()
    own = pl.ds(pl.multiple_of(c * TL, TL), TL)
    inputs = student[...].astype(F32)
    diag = eye(TL, 128)
    sums = jnp.sum(inputs * inputs, axis=1, keepdims=True)
    sq[...] = jnp.broadcast_to(
        jnp.sum(jnp.where(diag, sums, 0.0), axis=0, keepdims=True), (8, 128)
    )
    enter(me, c)
    sq_copies = exchange(
        "row", me, NR, lambda peer: sq, lambda d: sq_in.at[d - 1], sq_ss, sq_rs
    )
    loads[0].wait()
    for i in range(4):
        product = jnp.dot(
            teacher[...], proj_v[:, i * 4 * DL : (i + 1) * 4 * DL], preferred_element_type=F32
        )
        for j in range(4):
            tpart[i * 4 + j] = product[:, j * DL : (j + 1) * DL].astype(BF16)
    t_copies = exchange(
        "row", me, NR, lambda peer: tpart.at[peer], lambda d: tpart_in.at[d - 1], t_ss, t_rs
    )
    for copy in sq_copies:
        copy.wait_recv()
    total = sq[0:1] + jnp.sum(sq_in[:, 0, :], axis=0, keepdims=True)
    mean_sq = jnp.sum(jnp.where(diag, total, 0.0), axis=1, keepdims=True) / D
    inv_rms = 1.0 / jnp.sqrt(mean_sq + 1e-06)
    normed[own, :] = (inputs * inv_rms * gain[...].astype(F32)).astype(BF16)
    n_copies = exchange(
        "col", c, NC, lambda peer: normed.at[own, :], lambda d: normed.at[own, :], n_ss, n_rs
    )
    for copy in n_copies:
        copy.wait_recv()
    loads[1].wait()
    loads[2].wait()

    xp, xm = lax.rem(x + 1, 4) * 4 + z, lax.rem(x + 3, 4) * 4 + z
    zp, zm = x * 4 + lax.rem(z + 1, 4), x * 4 + lax.rem(z + 3, 4)
    first = ((x, xp, xm), (z, zp, zm))
    second = ((z, zp, zm), (x, xp, xm))
    scatter1 = [
        Scatter(part, 64, s * FL, FL, *first[s], recv1.at[s], acc1.at[s], s_ss.at[s], s_rs.at[s])
        for s in range(2)
    ]
    scatter2 = [
        Scatter(
            mid.at[s], 16, 0, FL, *second[s], recv2.at[s], acc2.at[s],
            s_ss.at[2 + s], s_rs.at[2 + s],
        )
        for s in range(2)
    ]
    for s in range(2):
        @pl.loop(0, FH // TILE)
        def _(i):
            source = pl.ds(pl.multiple_of(s * FH + i * TILE, 128), TILE)
            to_gate = pl.ds(pl.multiple_of(s * FL + i * TILE, 128), TILE)
            to_up = pl.ds(pl.multiple_of(s * FL + FH + i * TILE, 128), TILE)
            rows = normed[...]
            part[:, to_gate] = jnp.dot(
                rows, wg_v[:, source], preferred_element_type=F32
            ).astype(BF16)
            part[:, to_up] = jnp.dot(
                rows, wu_v[:, source], preferred_element_type=F32
            ).astype(BF16)
        scatter1[s].start()
    for s in range(2):
        scatter1[s].relay()
    for s in range(2):
        a, b = scatter1[s].result()
        mid[s, :, 0:FH] = a.astype(BF16)
        mid[s, :, FH:FL] = b.astype(BF16)
        scatter2[s].start()
    for s in range(2):
        scatter2[s].relay()
    gather1, gather2 = [], []
    for s in range(2):
        gate, up = scatter2[s].result()
        act, slope = gelu_pair(gate)
        act_v[s] = act
        ups_v[s] = up * slope
        p1, p2 = first[s], second[s]
        base = pl.multiple_of(p1[0] * 64, 64)
        at = pl.multiple_of(base + p2[0] * 16, 16)
        hidden[pl.ds(at, 16), s * FH : (s + 1) * FH] = (act * up).astype(BF16)
        gather1.append(
            Gather(hidden, base, 16, s * FH, FH, *p2, g_ss.at[s], g_rs.at[s])
        )
        gather2.append(
            Gather(hidden, 0, 64, s * FH, FH, *p1, g_ss.at[2 + s], g_rs.at[2 + s])
        )
        gather1[s].start()
    for s in range(2):
        gather1[s].relay()
    for s in range(2):
        gather1[s].done()
        gather2[s].start()
    for s in range(2):
        gather2[s].relay()
    finish(t_copies)
    target = tpart[me].astype(F32)
    for d in range(NR - 1):
        target = target + tpart_in[d].astype(F32)
    target = target.astype(BF16).astype(F32)
    loads[3].wait()
    for s in range(2):
        gather2[s].done()
    hidden_copy = pltpu.make_async_copy(hidden, hidden_out, out_sem.at[0])
    hidden_copy.start()
    normed_copy = pltpu.make_async_copy(normed, normed_out, out_sem.at[1])
    normed_copy.start()

    down_acc[...] = jnp.zeros_like(down_acc)

    @pl.loop(0, FL // TILE)
    def _(i):
        lanes = pl.ds(pl.multiple_of(i * TILE, 128), TILE)
        down_acc[...] += lax.dot_general(
            hidden[:, lanes], wd_v[:, lanes], (((1,), (1,)), ((), ())),
            preferred_element_type=F32,
        )

    down_part[...] = down_acc[...].astype(BF16)
    d_copies = exchange(
        "col", c, NC,
        lambda peer: down_part.at[pl.ds(pl.multiple_of(peer * TL, TL), TL), :],
        lambda d: down_in.at[d - 1], d_ss, d_rs,
    )
    for copy in d_copies:
        copy.wait_recv()
    down = down_acc[own, :]
    for d in range(NC - 1):
        down = down + down_in[d].astype(F32)
    residue = inputs + down - target
    loss = jnp.sum(residue * residue)
    loss_out[...] = jnp.zeros_like(loss_out) + loss
    dy[own, :] = (residue / TOKENS).astype(BF16)
    y_copies = exchange(
        "col", c, NC, lambda peer: dy.at[own, :], lambda d: dy.at[own, :], y_ss, y_rs
    )
    for copy in y_copies:
        copy.wait_recv()
    dy_copy = pltpu.make_async_copy(dy, dy_out, out_sem.at[2])
    dy_copy.start()

    gscatter1 = [
        Scatter(
            gpart, 64, s * FH, FH, *first[s], grecv1.at[s], gacc1.at[s],
            s_ss.at[4 + s], s_rs.at[4 + s],
        )
        for s in range(2)
    ]
    gscatter2 = [
        Scatter(
            gmid.at[s], 16, 0, FH, *second[s], grecv2.at[s], gacc2.at[s],
            s_ss.at[6 + s], s_rs.at[6 + s],
        )
        for s in range(2)
    ]
    for s in range(2):
        @pl.loop(0, FH // TILE)
        def _(i):
            lanes = pl.ds(pl.multiple_of(s * FH + i * TILE, 128), TILE)
            gpart[:, lanes] = jnp.dot(
                dy[...], wd_v[:, lanes], preferred_element_type=F32
            ).astype(BF16)
        gscatter1[s].start()
    for s in range(2):
        gscatter1[s].relay()
    for s in range(2):
        a, b = gscatter1[s].result()
        gmid[s, :, 0 : FH // 2] = a.astype(BF16)
        gmid[s, :, FH // 2 : FH] = b.astype(BF16)
        gscatter2[s].start()
    for s in range(2):
        gscatter2[s].relay()
    ggather1, ggather2 = [], []
    for s in range(2):
        halves = gscatter2[s].result()
        p1, p2 = first[s], second[s]
        base = pl.multiple_of(p1[0] * 64, 64)
        at = pl.ds(pl.multiple_of(base + p2[0] * 16, 16), 16)
        for h in range(2):
            lo = h * (FH // 2)
            hi = lo + FH // 2
            grads[at, s * FL + lo : s * FL + hi] = (halves[h] * ups_v[s, :, lo:hi]).astype(BF16)
            grads[at, s * FL + FH + lo : s * FL + FH + hi] = (
                halves[h] * act_v[s, :, lo:hi]
            ).astype(BF16)
        ggather1.append(
            Gather(grads, base, 16, s * FL, FL, *p2, g_ss.at[4 + s], g_rs.at[4 + s])
        )
        ggather2.append(
            Gather(grads, 0, 64, s * FL, FL, *p1, g_ss.at[6 + s], g_rs.at[6 + s])
        )
        ggather1[s].start()
    for s in range(2):
        ggather1[s].relay()
    for s in range(2):
        ggather1[s].done()
        ggather2[s].start()
    for s in range(2):
        ggather2[s].relay()
    for s in range(2):
        ggather2[s].done()
    grads_copy = pltpu.make_async_copy(grads, grads_out, out_sem.at[3])
    grads_copy.start()
    for copy in sq_copies + n_copies + d_copies + y_copies:
        copy.wait_send()
    for group in (scatter1, scatter2, gscatter1, gscatter2, gather1, gather2, ggather1, ggather2):
        for one in group:
            one.drain()
    for copy in (hidden_copy, normed_copy, dy_copy, grads_copy):
        copy.wait()


def whole(space=pltpu.VMEM):
    return pl.BlockSpec(memory_space=space)


def step(teacher, projection, student, gain, w_gate, w_up, w_down):
    sem = pltpu.SemaphoreType.DMA
    q = FH // 2
    return pl.pallas_call(
        step_kernel,
        out_shape=(
            jax.ShapeDtypeStruct((TOKENS, DL), BF16),
            jax.ShapeDtypeStruct((TOKENS, DL), BF16),
            jax.ShapeDtypeStruct((TOKENS, FL), BF16),
            jax.ShapeDtypeStruct((TOKENS, 2 * FL), BF16),
            jax.ShapeDtypeStruct((8, 128), F32),
        ),
        in_specs=[
            whole(), whole(pl.ANY), whole(), whole(), whole(pl.ANY), whole(pl.ANY), whole(pl.ANY)
        ],
        out_specs=(whole(pl.ANY), whole(pl.ANY), whole(pl.ANY), whole(pl.ANY), whole()),
        scratch_shapes=[
            pltpu.VMEM(projection.shape, BF16),
            pltpu.VMEM((DL, FL), BF16),
            pltpu.VMEM((DL, FL), BF16),
            pltpu.VMEM((DL, FL), BF16),
            pltpu.VMEM((8, 128), F32),
            pltpu.VMEM((NR - 1, 8, 128), F32),
            pltpu.VMEM((NR, TL, DL), BF16),
            pltpu.VMEM((NR - 1, TL, DL), BF16),
            pltpu.VMEM((TOKENS, DL), BF16),
            pltpu.VMEM((TOKENS, 2 * FL), BF16),
            pltpu.VMEM((2, 64, FL), BF16),
            pltpu.VMEM((2, 6, 64, FH), BF16),
            pltpu.VMEM((2, 2, 64, FH), BF16),
            pltpu.VMEM((2, 6, 16, FH), BF16),
            pltpu.VMEM((2, 2, 16, FH), BF16),
            pltpu.VMEM((TOKENS, FL), BF16),
            pltpu.VMEM((2, 16, FH), F32),
            pltpu.VMEM((2, 16, FH), F32),
            pltpu.VMEM((TOKENS, DL), F32),
            pltpu.VMEM((TOKENS, DL), BF16),
            pltpu.VMEM((NC - 1, TL, DL), BF16),
            pltpu.VMEM((TOKENS, DL), BF16),
            pltpu.VMEM((TOKENS, FL), BF16),
            pltpu.VMEM((2, 64, FH), BF16),
            pltpu.VMEM((2, 6, 64, q), BF16),
            pltpu.VMEM((2, 2, 64, q), BF16),
            pltpu.VMEM((2, 6, 16, q), BF16),
            pltpu.VMEM((2, 2, 16, q), BF16),
            pltpu.VMEM((TOKENS, 2 * FL), BF16),
            sem((4,)), sem((4,)),
            sem((NR - 1,)), sem((NR - 1,)), sem((NR - 1,)), sem((NR - 1,)),
            sem((NC - 1,)), sem((NC - 1,)), sem((NC - 1,)), sem((NC - 1,)),
            sem((NC - 1,)), sem((NC - 1,)),
            sem((8, 6)), sem((8, 6)), sem((8, 4)), sem((8, 4)),
        ],
        compiler_params=pltpu.CompilerParams(
            collective_id=0, has_side_effects=True, vmem_limit_bytes=VMEM_LIMIT
        ),
        name="step",
    )(teacher, projection, student, gain, w_gate, w_up, w_down)


def stats_kernel(
    normed, dy, hidden, grads, row_old, col_old, loss_in,
    row_out, col_out, total_out,
    left, values, racc, csend, cin, cfull, rsend, rin, cflat, cinv, qsend, qin, qmid, qmid_in,
    c_ss, c_rs, a_ss, a_rs, r_ss, r_rs, q_ss, q_rs, l_ss, l_rs,
):
    me = lax.axis_index("row")
    c = lax.axis_index("col")
    tiles = FL // TILE
    rows_per = TILE // 128
    csend[...] = jnp.zeros_like(csend)
    racc[...] = jnp.zeros_like(racc)
    left[0] = normed[...].astype(F32).T.astype(BF16)
    left[1] = dy[...].astype(F32).T.astype(BF16)

    def tile(m, i):
        lanes = pl.ds(pl.multiple_of(i * TILE, 128), TILE)
        if m == 2:
            return lanes, left[1], hidden[:, lanes]
        at = i * TILE + m * FH + lax.div(i, tiles // 2) * FH
        return lanes, left[0], grads[:, pl.ds(pl.multiple_of(at, 128), TILE)]

    for m in range(3):
        @pl.loop(0, tiles)
        def _(i):
            lanes, lhs, rhs = tile(m, i)
            grad = jnp.dot(lhs, rhs, preferred_element_type=F32)
            values[m, :, lanes] = grad
            square = grad * grad
            folded = square[:, 0:128]
            for k in range(1, rows_per):
                folded = folded + square[:, k * 128 : (k + 1) * 128]
            racc[m] += folded
            down = jnp.sum(square, axis=0, keepdims=True)
            for k in range(rows_per):
                csend[pl.ds(m * (FL // 128) + i * rows_per + k, 1), :] = down[
                    :, k * 128 : (k + 1) * 128
                ]

    diag = eye(DL, DL)
    rsend[...] = jnp.zeros_like(rsend)
    for m in range(3):
        sums = jnp.sum(racc[m], axis=1, keepdims=True)
        rsend[m : m + 1, :] = jnp.sum(jnp.where(diag, sums, 0.0), axis=0, keepdims=True)
    enter(me, c)
    c_copies = exchange(
        "row", me, NR,
        lambda peer: csend.at[pl.ds(pl.multiple_of(peer * 8, 8), 8), :],
        lambda d: cin.at[d - 1], c_ss, c_rs,
    )
    r_copies = exchange(
        "col", c, NC, lambda peer: rsend, lambda d: rin.at[d - 1], r_ss, r_rs
    )
    mine = pl.ds(pl.multiple_of(me * 8, 8), 8)
    for copy in c_copies:
        copy.wait_recv()
    cfull[mine, :] = csend[mine, :] + jnp.sum(cin[...], axis=0)
    a_copies = exchange(
        "row", me, NR, lambda peer: cfull.at[mine, :], lambda d: cfull.at[mine, :], a_ss, a_rs
    )
    for copy in r_copies:
        copy.wait_recv()
    row_sum = rsend[...] + jnp.sum(rin[...], axis=0)
    row_new = 0.8 * row_old[...] + 0.2 * (row_sum[0:3] / FF + 1e-30)
    row_out[...] = row_new
    for copy in a_copies:
        copy.wait_recv()
    for m in range(3):
        for k in range(FL // 128):
            at = m * (FL // 128) + k
            cflat[m : m + 1, k * 128 : (k + 1) * 128] = cfull[at : at + 1, :]
    col_new = 0.8 * col_old[...] + 0.2 * (cflat[...] / D + 1e-30)
    col_out[...] = col_new
    cinv[...] = 1.0 / col_new
    row_inv = 1.0 / row_new
    racc[...] = jnp.zeros_like(racc)
    for m in range(3):
        @pl.loop(0, tiles)
        def _(i):
            lanes = pl.ds(pl.multiple_of(i * TILE, 128), TILE)
            grad = values[m, :, lanes]
            square = grad * grad * cinv[m : m + 1, lanes]
            folded = square[:, 0:128]
            for k in range(1, rows_per):
                folded = folded + square[:, k * 128 : (k + 1) * 128]
            racc[m] += folded
        column = jnp.sum(jnp.where(diag, row_inv[m : m + 1], 0.0), axis=1, keepdims=True)
        qsend[m : m + 1, :] = jnp.sum(racc[m] * column, axis=0, keepdims=True)
    qsend[3:8, :] = loss_in[3:8, :]
    q_copies = exchange(
        "row", me, NR, lambda peer: qsend, lambda d: qin.at[d - 1], q_ss, q_rs
    )
    for copy in q_copies:
        copy.wait_recv()
    qmid[...] = qsend[...] + jnp.sum(qin[...], axis=0)
    l_copies = exchange(
        "col", c, NC, lambda peer: qmid, lambda d: qmid_in.at[d - 1], l_ss, l_rs
    )
    for copy in l_copies:
        copy.wait_recv()
    total_out[...] = qmid[...] + jnp.sum(qmid_in[...], axis=0)
    for copy in c_copies + r_copies + a_copies + q_copies + l_copies:
        copy.wait_send()


def stats(normed, dy, hidden, grads, row_old, col_old, loss):
    sem = pltpu.SemaphoreType.DMA
    return pl.pallas_call(
        stats_kernel,
        out_shape=(
            jax.ShapeDtypeStruct((3, DL), F32),
            jax.ShapeDtypeStruct((3, FL), F32),
            jax.ShapeDtypeStruct((8, 128), F32),
        ),
        in_specs=[whole()] * 7,
        out_specs=(whole(),) * 3,
        scratch_shapes=[
            pltpu.VMEM((2, DL, TOKENS), BF16),
            pltpu.VMEM((3, DL, FL), F32),
            pltpu.VMEM((3, DL, 128), F32),
            pltpu.VMEM((128, 128), F32),
            pltpu.VMEM((NR - 1, 8, 128), F32),
            pltpu.VMEM((128, 128), F32),
            pltpu.VMEM((8, DL), F32),
            pltpu.VMEM((NC - 1, 8, DL), F32),
            pltpu.VMEM((3, FL), F32),
            pltpu.VMEM((3, FL), F32),
            pltpu.VMEM((8, 128), F32),
            pltpu.VMEM((NR - 1, 8, 128), F32),
            pltpu.VMEM((8, 128), F32),
            pltpu.VMEM((NC - 1, 8, 128), F32),
            sem((NR - 1,)), sem((NR - 1,)), sem((NR - 1,)), sem((NR - 1,)),
            sem((NC - 1,)), sem((NC - 1,)), sem((NR - 1,)), sem((NR - 1,)),
            sem((NC - 1,)), sem((NC - 1,)),
        ],
        compiler_params=pltpu.CompilerParams(
            collective_id=1, has_side_effects=True, vmem_limit_bytes=VMEM_LIMIT
        ),
        name="stats",
    )(normed, dy, hidden, grads, row_old, col_old, loss)


def update_kernel(normed, dy, hidden, gate_in, up_in, row_new, col_new, total, out0, out1, out2, left, scale):
    @pl.when(pl.program_id(0) == 0)
    def _():
        left[0] = normed[...].astype(F32).T.astype(BF16)
        left[1] = dy[...].astype(F32).T.astype(BF16)
        diag = eye(DL, DL)
        for m in range(3):
            mean = jnp.sum(total[m : m + 1, :], axis=1, keepdims=True) / (float(D) * FF)
            clip = 1.0 / jnp.maximum(1.0, jnp.sqrt(mean))
            column = jnp.sum(
                jnp.where(diag, row_new[m : m + 1, :], 0.0), axis=1, keepdims=True
            )
            scale[m] = jnp.broadcast_to(clip / jnp.sqrt(column), (DL, 128))

    for m, (lhs, rhs, out) in enumerate(
        ((left[0], gate_in, out0), (left[0], up_in, out1), (left[1], hidden, out2))
    ):
        grad = jnp.dot(lhs, rhs[...], preferred_element_type=F32)
        lane = 1.0 / jnp.sqrt(col_new[m : m + 1, :])
        for k in range(TILE // 128):
            at = slice(k * 128, (k + 1) * 128)
            out[:, at] = (grad[:, at] * scale[m] * lane[:, at]).astype(BF16)


def update(normed, dy, hidden, grads, row_new, col_new, total):
    full = lambda shape: pl.BlockSpec(shape, lambda i: (0, 0))
    tile = pl.BlockSpec((DL, TILE), lambda i: (0, i))
    half = FH // TILE
    return pl.pallas_call(
        update_kernel,
        grid=(FL // TILE,),
        out_shape=(jax.ShapeDtypeStruct((DL, FL), BF16),) * 3,
        in_specs=[
            full((TOKENS, DL)),
            full((TOKENS, DL)),
            pl.BlockSpec((TOKENS, TILE), lambda i: (0, i)),
            pl.BlockSpec((TOKENS, TILE), lambda i: (0, i + lax.div(i, half) * half)),
            pl.BlockSpec((TOKENS, TILE), lambda i: (0, i + half + lax.div(i, half) * half)),
            full((3, DL)),
            pl.BlockSpec((3, TILE), lambda i: (0, i)),
            full((8, 128)),
        ],
        out_specs=(tile,) * 3,
        scratch_shapes=[pltpu.VMEM((2, DL, TOKENS), BF16), pltpu.VMEM((3, DL, 128), F32)],
        compiler_params=pltpu.CompilerParams(dimension_semantics=("arbitrary",)),
        name="update",
    )(normed, dy, hidden, grads, grads, row_new, col_new, total)


def shards(teacher_rows, projection, student_in, norm_gain, w_gate, w_up, w_down, row_old, col_old):
    normed, dy, hidden, grads, loss = step(
        teacher_rows, projection, student_in, norm_gain[None, :], w_gate, w_up, w_down
    )
    row_new, col_new, total = stats(normed, dy, hidden, grads, row_old, col_old, loss)
    out = update(normed, dy, hidden, grads, row_new, col_new, total)
    return (*out, row_new, col_new, 0.5 * total[3, 0] / TOKENS)


def solution(mesh):
    placed = (
        P("col", "row"),
        P("row", None),
        P("col", "row"),
        P("row"),
        P("row", "col"),
        P("row", "col"),
        P("row", "col"),
        P(None, "row"),
        P(None, "col"),
    )
    return jax.shard_map(
        shards,
        mesh=mesh,
        in_specs=placed,
        out_specs=(
            P("row", "col"),
            P("row", "col"),
            P("row", "col"),
            P(None, "row"),
            P(None, "col"),
            P(),
        ),
        check_vma=False,
    )
```

time: 662 us -> 190 us (0.29)
  waiting for transfers between devices: 343 us -> 0 us
  blocking collectives: 222 us -> 0 us
  Pallas kernels: 0 us -> 184 us
  matrix products: 39.8 us -> 0 us
  other arithmetic: 34.5 us -> 0 us
  between operations: 17.8 us -> 2.46 us
    psum x2 -> x0, waiting for transfers between devices: 241 us -> none  [the longest x1 139 us: shards(): gate_sum, up_sum = lax.psum((gate_part, up_part), 'row')]
    psum x4 -> x0, blocking collectives: 185 us -> none  [the longest x1 78.3 us: shards(): lax.psum((update_sums[0], update_sums[1], update_sums[2]), ('row', 'col'))]
    pallas_call x0 -> x3, Pallas kernels: none -> 184 us  [the longest x1 135 us: step(): pl.pallas_call(step_kernel, out_shape=(jax.ShapeDtypeStruct((TOKENS, DL),...]
    unnamed x5 -> x0, waiting for transfers between devices: 69.8 us -> none
    all_gather x2 -> x0, blocking collectives: 37 us -> none  [the longest x1 20.9 us: shards(): normed_all = lax.all_gather(normed, 'col', axis=0, tiled=True)]
    dot_general x7 -> x0, matrix products: 34.1 us -> none  [the longest x1 8.95 us: shards(): lax.dot_general(normed_all, grad_gatein, (((0,), (0,)), ((), ())), prefer...]
    reduce_scatter x1 -> x0, waiting for transfers between devices: 31.4 us -> none  [shards(): lax.psum_scatter(lax.dot_general(hidden, w_down, (((1,), (1,)), ((), ()))...]
    convert_element_type x6 -> x0, other arithmetic: 21.2 us -> none  [the longest x3 14.8 us: shards(): (updates[which] / jnp.maximum(1.0, jnp.sqrt(totals[which] / (D * FF)))).a...]
  transfers between devices with their start and end apart: 4 -> 0, of which waited for: 4 -> 0; matrix products, arithmetic and copies ran while one was open for 3% -> 0% of each run, Pallas kernels for 0% -> 0%
where the time goes in v1:
time: 190 us
  Pallas kernels  184 us (97%)
  local copies, waits for them, and re-layouts  3.66 us (2%)
  between operations  2.46 us (1%)
    pallas_call x1, Pallas kernels, step(): pl.pallas_call(step_kernel, out_shape=(jax.ShapeDtypeStruct((TOKENS, DL),...  135 us
    pallas_call x1, Pallas kernels, stats(): pl.pallas_call(stats_kernel, out_shape=(jax.ShapeDtypeStruct((3, DL), F32...  39.4 us
    pallas_call x1, Pallas kernels, update(): pl.pallas_call(update_kernel, grid=(FL // TILE,), out_shape=(jax.ShapeDty...  8.86 us

profile of v1, /device:TPU:1, one launch (start us, length us, event | category | flops | bytes accessed | tf_op | source)
XLA Modules:
  0.0 189.7 jit_solution(6571262519362515597)
XLA Ops:
  0.6 1.2 broadcast_in_dim.3.gain
  1.9 135.3 %step.1 = (bf16[256,288]{1,0:T(8,128)(2,1)}, bf16[256,288]{1,0:T(8,128)(2,1)}, bf16[256,4608]{1,0:T(8,128)(2,1)}, bf16[256,9216]{1,0:T(8,128)(2,1)}, f32[8,128]{1,0:T(8,128)}) custom-call(bf16[32,512]{1,0:T(8,128)(2,1)} %teacher.1, bf16[512,4608]{1,0:T(8,128)(2,1)} %projection.1, bf16[32,288]{1,0:T(8,128)(2,1)} %student.1, ...), custom_call_target="tpu_custom_call" | custom-call | tf_op jit(solution)/shard_map/step/pallas_call | solution.py:408
  137.2 39.4 %stats.1 = (f32[3,288]{1,0:T(4,128)}, f32[3,4608]{1,0:T(4,128)}, f32[8,128]{1,0:T(8,128)}) custom-call(bf16[256,288]{1,0:T(8,128)(2,1)} %get-tuple-element.17.normed, bf16[256,288]{1,0:T(8,128)(2,1)} %get-tuple-element.18.dy, bf16[256,4608]{1,0:T(8,128)(2,1)} %get-tuple-element.19.hidden, bf16[256,9216]{1,0:T(8,128)(2,1)} %get-tuple-element.20.grads.gate_in.up_in, ...), custom_call_target="tpu_custom_call" | custom-call | tf_op jit(solution)/shard_map/stats/pallas_call | solution.py:571
  176.6 0.0 copy-start.1
  176.6 0.0 copy-start
  176.6 8.9 %update.1 = (bf16[288,4608]{1,0:T(8,128)(2,1)}, bf16[288,4608]{1,0:T(8,128)(2,1)}, bf16[288,4608]{1,0:T(8,128)(2,1)}) custom-call(bf16[256,288]{1,0:T(8,128)(2,1)} %get-tuple-element.17.normed, bf16[256,288]{1,0:T(8,128)(2,1)} %get-tuple-element.18.dy, bf16[256,4608]{1,0:T(8,128)(2,1)} %get-tuple-element.19.hidden, ...), custom_call_target="tpu_custom_call" | custom-call | tf_op jit(solution)/shard_map/update/pallas_call | solution.py:634
  185.5 1.2 slice.3
  187.3 0.0 copy-done.1
  187.3 0.6 copy.17
  187.9 0.0 copy-done
  187.9 0.6 copy.18
Async XLA Ops:
  176.6 10.7 %copy-start.1 = (f32[3,288]{1,0:T(4,128)S(1)}, f32[3,288]{1,0:T(4,128)}, u32[]{:S(2)}) copy-start(f32[3,288]{1,0:T(4,128)} %get-tuple-element.37.row_new) | copy-start | bytes 10372
  176.6 11.3 %copy-start = (f32[3,4608]{1,0:T(4,128)S(1)}, f32[3,4608]{1,0:T(4,128)}, u32[]{:S(2)}) copy-start(f32[3,4608]{1,0:T(4,128)} %get-tuple-element.38.col_new) | copy-start | bytes 165892

commit v2 on v1

v2 whole, which is shorter than its diff:
```python
import math

import jax
import jax.numpy as jnp
from jax import lax
from jax.experimental import pallas as pl
from jax.experimental.pallas import tpu as pltpu
from jax.sharding import PartitionSpec as P

D = 4608
FF = 36864
TOKENS = 256
NR = 16
NC = 8
DL = D // NR
FL = FF // NC
TL = TOKENS // NC
TILE = 768
F32 = jnp.float32
BF16 = jnp.bfloat16
VMEM_LIMIT = 67_000_000


def gelu_pair(values):
    root_coef = math.sqrt(2.0 / math.pi)
    tangent = jnp.tanh(root_coef * (values + 0.044715 * values * values * values))
    gelu_val = 0.5 * values * (1.0 + tangent)
    gelu_slope = 0.5 * (1.0 + tangent) + 0.5 * values * (1.0 - tangent * tangent) * root_coef * (
        1.0 + 3.0 * 0.044715 * values * values
    )
    return (gelu_val, gelu_slope)


def remote(src, dst, send_sem, recv_sem, axis, index):
    return pltpu.make_async_remote_copy(
        src_ref=src,
        dst_ref=dst,
        send_sem=send_sem,
        recv_sem=recv_sem,
        device_id={axis: index},
        device_id_type=pl.DeviceIdType.MESH,
    )


def greet(me, c):
    barrier = pltpu.get_barrier_semaphore()
    for d in range(1, NR):
        pl.semaphore_signal(
            barrier, inc=1, device_id={"row": lax.rem(me + d, NR)},
            device_id_type=pl.DeviceIdType.MESH,
        )
    for d in range(1, NC):
        pl.semaphore_signal(
            barrier, inc=1, device_id={"col": lax.rem(c + d, NC)},
            device_id_type=pl.DeviceIdType.MESH,
        )


def met():
    pl.semaphore_wait(pltpu.get_barrier_semaphore(), NR + NC - 2)


def exchange(axis, me, n, source, slots, send_sem, recv_sem):
    copies = []
    for d in range(1, n):
        peer = lax.rem(me + d, n)
        copy = remote(
            source(peer), slots(d), send_sem.at[d - 1], recv_sem.at[d - 1], axis, peer
        )
        copy.start()
        copies.append(copy)
    return copies


def finish(copies):
    for copy in copies:
        copy.wait_recv()
    for copy in copies:
        copy.wait_send()


class Scatter:
    def __init__(self, buf, wide, rows, lo, wide_lo, width, p, plus, minus, recv, acc, ss, rs):
        self.buf, self.wide, self.rows = buf, wide, rows
        self.lo, self.wide_lo, self.half = lo, wide_lo, width // 2
        self.p, self.plus, self.minus = p, plus, minus
        self.recv, self.acc, self.ss, self.rs = recv, acc, ss, rs

    def part(self, k, which):
        at = pl.multiple_of(lax.rem(self.p + k, 4) * self.rows, 16)
        return self.buf.at[pl.ds(at, self.rows), pl.ds(self.lo + which * self.half, self.half)]

    def own(self, k, which):
        at = pl.multiple_of(lax.rem(self.p + k, 4) * self.rows, 16)
        return self.wide[pl.ds(at, self.rows), pl.ds(self.wide_lo + which * self.half, self.half)]

    def send(self, src, slot, to):
        copy = remote(
            src, self.recv.at[slot], self.ss.at[slot], self.rs.at[slot], "row", to
        )
        copy.start()
        return copy

    def start(self):
        self.copies = [
            self.send(self.part(2, 0), 0, self.plus),
            self.send(self.part(2, 1), 1, self.minus),
            self.send(self.part(1, 1), 2, self.plus),
            self.send(self.part(3, 0), 3, self.minus),
        ]

    def relay(self):
        self.copies[0].wait_recv()
        self.acc[0] = (self.own(1, 0) + self.recv[0].astype(F32)).astype(BF16)
        self.copies.append(self.send(self.acc.at[0], 4, self.plus))
        self.copies[1].wait_recv()
        self.acc[1] = (self.own(3, 1) + self.recv[1].astype(F32)).astype(BF16)
        self.copies.append(self.send(self.acc.at[1], 5, self.minus))

    def result(self):
        for at in (3, 2, 4, 5):
            self.copies[at].wait_recv()
        first = self.own(0, 0) + self.recv[3].astype(F32) + self.recv[4].astype(F32)
        second = self.own(0, 1) + self.recv[2].astype(F32) + self.recv[5].astype(F32)
        return (first, second)

    def drain(self):
        for copy in self.copies:
            copy.wait_send()


class Gather:
    def __init__(self, buf, base, rows, lo, width, p, plus, minus, ss, rs):
        self.buf, self.base, self.rows, self.lo, self.width = buf, base, rows, lo, width
        self.p, self.plus, self.minus, self.ss, self.rs = p, plus, minus, ss, rs

    def part(self, k, lo, width):
        at = pl.multiple_of(self.base + lax.rem(self.p + k, 4) * self.rows, 16)
        return self.buf.at[pl.ds(at, self.rows), pl.ds(self.lo + lo, width)]

    def send(self, ref, slot, to):
        copy = remote(ref, ref, self.ss.at[slot], self.rs.at[slot], "row", to)
        copy.start()
        return copy

    def start(self):
        self.copies = [
            self.send(self.part(0, 0, self.width), 0, self.plus),
            self.send(self.part(0, 0, self.width), 1, self.minus),
        ]

    def relay(self):
        half = self.width // 2
        self.copies[0].wait_recv()
        self.copies.append(self.send(self.part(3, 0, half), 2, self.plus))
        self.copies[1].wait_recv()
        self.copies.append(self.send(self.part(1, half, half), 3, self.minus))

    def done(self):
        self.copies[2].wait_recv()
        self.copies[3].wait_recv()

    def drain(self):
        for copy in self.copies:
            copy.wait_send()


def eye(rows, lanes):
    return lax.broadcasted_iota(jnp.int32, (rows, lanes), 0) == lax.broadcasted_iota(
        jnp.int32, (rows, lanes), 1
    )


def step_kernel(
    teacher, projection, student, gain, w_gate, w_up, w_down, row_old, col_old,
    normed_out, dy_out, hidden_out, grads_out, row_out, col_out, total_out,
    proj_v, wg_v, wu_v, wd_v, sq, sq_in, tpart, tpart_in, normed, part, mid, mid32, recv1, acc1,
    recv2, acc2, hidden, act_v, ups_v, down_acc, down_part, down_in, dy, gpart, gmid, gmid32,
    grecv1, gacc1, grecv2, gacc2, grads, big,
    left, racc, csend, cin, cfull, rsend, rin, cflat, cinv, qsend, qin, qmid, qmid_in,
    load_sem, out_sem, sq_ss, sq_rs, t_ss, t_rs, n_ss, n_rs, d_ss, d_rs, y_ss, y_rs,
    s_ss, s_rs, g_ss, g_rs,
    c_ss, c_rs, a_ss, a_rs, r_ss, r_rs, q_ss, q_rs, l_ss, l_rs,
):
    me = lax.axis_index("row")
    c = lax.axis_index("col")
    x, z = lax.div(me, 4), lax.rem(me, 4)
    greet(me, c)
    loads = [
        pltpu.make_async_copy(src, dst, load_sem.at[i])
        for i, (src, dst) in enumerate(
            ((projection, proj_v), (w_gate, wg_v), (w_up, wu_v), (w_down, wd_v))
        )
    ]
    for load in loads:
        load.start()
    own = pl.ds(pl.multiple_of(c * TL, TL), TL)
    inputs = student[...].astype(F32)
    diag = eye(TL, 128)
    sums = jnp.sum(inputs * inputs, axis=1, keepdims=True)
    sq[...] = jnp.broadcast_to(
        jnp.sum(jnp.where(diag, sums, 0.0), axis=0, keepdims=True), (8, 128)
    )
    met()
    sq_copies = exchange(
        "row", me, NR, lambda peer: sq, lambda d: sq_in.at[d - 1], sq_ss, sq_rs
    )
    loads[0].wait()
    for i in range(4):
        product = jnp.dot(
            teacher[...], proj_v[:, i * 4 * DL : (i + 1) * 4 * DL], preferred_element_type=F32
        )
        for j in range(4):
            tpart[i * 4 + j] = product[:, j * DL : (j + 1) * DL].astype(BF16)
    t_copies = exchange(
        "row", me, NR, lambda peer: tpart.at[peer], lambda d: tpart_in.at[d - 1], t_ss, t_rs
    )
    for copy in sq_copies:
        copy.wait_recv()
    total = sq[0:1] + jnp.sum(sq_in[:, 0, :], axis=0, keepdims=True)
    mean_sq = jnp.sum(jnp.where(diag, total, 0.0), axis=1, keepdims=True) / D
    inv_rms = 1.0 / jnp.sqrt(mean_sq + 1e-06)
    normed[own, :] = (inputs * inv_rms * gain[...].astype(F32)).astype(BF16)
    n_copies = exchange(
        "col", c, NC, lambda peer: normed.at[own, :], lambda d: normed.at[own, :], n_ss, n_rs
    )
    for copy in n_copies:
        copy.wait_recv()
    for load in loads[1:]:
        load.wait()

    xp, xm = lax.rem(x + 1, 4) * 4 + z, lax.rem(x + 3, 4) * 4 + z
    zp, zm = x * 4 + lax.rem(z + 1, 4), x * 4 + lax.rem(z + 3, 4)
    first = ((x, xp, xm), (z, zp, zm))
    second = ((z, zp, zm), (x, xp, xm))
    drains = []

    def owner(s):
        base = pl.multiple_of(first[s][0] * 64, 64)
        return base, pl.ds(pl.multiple_of(base + second[s][0] * 16, 16), 16)

    def sub(lo, i):
        return pl.ds(pl.multiple_of(lo + i * 256, 128), 256)

    def run(stages):
        for t in range(len(stages) + 2):
            order = [j for j in range(3) if t == j] + [
                j for j in range(3) if 0 < t - j < len(stages)
            ]
            for j in order:
                for s in range(2):
                    stages[t - j](s, j)

    sc1, sc2, ga1, ga2 = {}, {}, {}, {}

    def f_start(s, j):
        k = 3 * s + j

        @pl.loop(0, 3)
        def _(i):
            rows = normed[...]
            for weights, off in ((wg_v, 0), (wu_v, TILE)):
                value = jnp.dot(rows, weights[:, sub(k * TILE, i)], preferred_element_type=F32)
                big[s * TOKENS : (s + 1) * TOKENS, sub(j * 2 * TILE + off, i)] = value
                part[:, sub(k * 2 * TILE + off, i)] = value.astype(BF16)

        sc1[k] = Scatter(
            part, big.at[s * TOKENS : (s + 1) * TOKENS], 64, k * 2 * TILE, j * 2 * TILE, 2 * TILE,
            *first[s], recv1.at[k], acc1.at[k], s_ss.at[k], s_rs.at[k],
        )
        sc1[k].start()
        drains.append(sc1[k])

    def f_relay1(s, j):
        sc1[3 * s + j].relay()

    def f_second(s, j):
        k = 3 * s + j
        for h, value in enumerate(sc1[k].result()):
            at = slice(h * TILE, (h + 1) * TILE)
            mid32[k, :, at] = value
            mid[k, :, at] = value.astype(BF16)
        sc2[k] = Scatter(
            mid.at[k], mid32.at[k], 16, 0, 0, 2 * TILE, *second[s], recv2.at[k], acc2.at[k],
            s_ss.at[6 + k], s_rs.at[6 + k],
        )
        sc2[k].start()
        drains.append(sc2[k])

    def f_relay2(s, j):
        sc2[3 * s + j].relay()

    def f_hidden(s, j):
        k = 3 * s + j
        gate, up = sc2[k].result()
        act, slope = gelu_pair(gate)
        act_v[k] = act
        ups_v[k] = up * slope
        base, rows = owner(s)
        hidden[rows, k * TILE : (k + 1) * TILE] = (act * up).astype(BF16)
        ga1[k] = Gather(hidden, base, 16, k * TILE, TILE, *second[s], g_ss.at[k], g_rs.at[k])
        ga1[k].start()
        drains.append(ga1[k])

    def f_relay3(s, j):
        ga1[3 * s + j].relay()

    def f_gather(s, j):
        k = 3 * s + j
        ga1[k].done()
        ga2[k] = Gather(
            hidden, 0, 64, k * TILE, TILE, *first[s], g_ss.at[6 + k], g_rs.at[6 + k]
        )
        ga2[k].start()
        drains.append(ga2[k])

    def f_relay4(s, j):
        ga2[3 * s + j].relay()

    down_acc[...] = jnp.zeros_like(down_acc)

    def f_down(s, j):
        k = 3 * s + j
        ga2[k].done()

        @pl.loop(0, 3)
        def _(i):
            lanes = sub(k * TILE, i)
            down_acc[...] += lax.dot_general(
                hidden[:, lanes], wd_v[:, lanes], (((1,), (1,)), ((), ())),
                preferred_element_type=F32,
            )

    run((f_start, f_relay1, f_second, f_relay2, f_hidden, f_relay3, f_gather, f_relay4, f_down))

    down_part[...] = down_acc[...].astype(BF16)
    d_copies = exchange(
        "col", c, NC,
        lambda peer: down_part.at[pl.ds(pl.multiple_of(peer * TL, TL), TL), :],
        lambda d: down_in.at[d - 1], d_ss, d_rs,
    )
    hidden_copy = pltpu.make_async_copy(hidden, hidden_out, out_sem.at[0])
    hidden_copy.start()
    normed_copy = pltpu.make_async_copy(normed, normed_out, out_sem.at[1])
    normed_copy.start()
    finish(t_copies)
    target = tpart[me].astype(F32)
    for d in range(NR - 1):
        target = target + tpart_in[d].astype(F32)
    rest = inputs - target.astype(BF16).astype(F32)
    for copy in d_copies:
        copy.wait_recv()
    down = down_acc[own, :]
    for d in range(NC - 1):
        down = down + down_in[d].astype(F32)
    residue = rest + down
    dy[own, :] = (residue / TOKENS).astype(BF16)
    y_copies = exchange(
        "col", c, NC, lambda peer: dy.at[own, :], lambda d: dy.at[own, :], y_ss, y_rs
    )
    qsend[...] = jnp.zeros_like(qsend) + jnp.sum(residue * residue)
    left[0] = normed[...].astype(F32).T.astype(BF16)
    for copy in y_copies:
        copy.wait_recv()
    dy_copy = pltpu.make_async_copy(dy, dy_out, out_sem.at[2])
    dy_copy.start()

    gs1, gs2, gg1, gg2 = {}, {}, {}, {}
    half = TILE // 2
    csend[...] = jnp.zeros_like(csend)
    racc[...] = jnp.zeros_like(racc)

    def b_start(s, j):
        k = 3 * s + j

        @pl.loop(0, 3)
        def _(i):
            lanes = sub(k * TILE, i)
            value = jnp.dot(dy[...], wd_v[:, lanes], preferred_element_type=F32)
            big[0:TOKENS, lanes] = value
            gpart[:, lanes] = value.astype(BF16)

        gs1[k] = Scatter(
            gpart, big.at[0:TOKENS], 64, k * TILE, k * TILE, TILE, *first[s],
            grecv1.at[k], gacc1.at[k], s_ss.at[12 + k], s_rs.at[12 + k],
        )
        gs1[k].start()
        drains.append(gs1[k])

    def b_relay1(s, j):
        gs1[3 * s + j].relay()

    def b_second(s, j):
        k = 3 * s + j
        for h, value in enumerate(gs1[k].result()):
            at = slice(h * half, (h + 1) * half)
            gmid32[k, :, at] = value
            gmid[k, :, at] = value.astype(BF16)
        gs2[k] = Scatter(
            gmid.at[k], gmid32.at[k], 16, 0, 0, TILE, *second[s], grecv2.at[k], gacc2.at[k],
            s_ss.at[18 + k], s_rs.at[18 + k],
        )
        gs2[k].start()
        drains.append(gs2[k])

    def b_relay2(s, j):
        gs2[3 * s + j].relay()

    def b_inputs(s, j):
        k = 3 * s + j
        base, rows = owner(s)
        for h, value in enumerate(gs2[k].result()):
            at = slice(h * half, (h + 1) * half)
            lo = 2 * k * TILE + h * half
            grads[rows, lo : lo + half] = (value * ups_v[k, :, at]).astype(BF16)
            lo = lo + TILE
            grads[rows, lo : lo + half] = (value * act_v[k, :, at]).astype(BF16)
        gg1[k] = Gather(
            grads, base, 16, 2 * k * TILE, 2 * TILE, *second[s], g_ss.at[12 + k], g_rs.at[12 + k]
        )
        gg1[k].start()
        drains.append(gg1[k])

    def b_relay3(s, j):
        gg1[3 * s + j].relay()

    def b_gather(s, j):
        k = 3 * s + j
        gg1[k].done()
        gg2[k] = Gather(
            grads, 0, 64, 2 * k * TILE, 2 * TILE, *first[s], g_ss.at[18 + k], g_rs.at[18 + k]
        )
        gg2[k].start()
        drains.append(gg2[k])

    def b_relay4(s, j):
        gg2[3 * s + j].relay()

    def sums_of(m, k, rhs, lo):
        @pl.loop(0, 3)
        def _(i):
            grad = jnp.dot(left[m // 2], rhs[:, sub(lo, i)], preferred_element_type=F32)
            big[m * DL : (m + 1) * DL, sub(k * TILE, i)] = grad
            square = grad * grad
            racc[m] += square[:, 0:128] + square[:, 128:256]
            column = jnp.sum(square, axis=0, keepdims=True)
            for n in range(2):
                csend[pl.ds(m * (FL // 128) + k * 6 + i * 2 + n, 1), :] = column[
                    :, n * 128 : (n + 1) * 128
                ]

    def b_sums(s, j):
        k = 3 * s + j
        gg2[k].done()
        sums_of(0, k, grads, 2 * k * TILE)
        sums_of(1, k, grads, (2 * k + 1) * TILE)

    def b_relay1_and_down(s, j):
        if s == 0 and j == 0:
            left[1] = dy[...].astype(F32).T.astype(BF16)
        b_relay1(s, j)
        sums_of(2, 3 * s + j, hidden, (3 * s + j) * TILE)

    run(
        (
            b_start, b_relay1_and_down, b_second, b_relay2, b_inputs, b_relay3, b_gather,
            b_relay4, b_sums,
        )
    )
    grads_copy = pltpu.make_async_copy(grads, grads_out, out_sem.at[3])
    grads_copy.start()

    c_copies = exchange(
        "row", me, NR,
        lambda peer: csend.at[pl.ds(pl.multiple_of(peer * 8, 8), 8), :],
        lambda d: cin.at[d - 1], c_ss, c_rs,
    )
    wide = eye(DL, DL)
    rsend[...] = jnp.zeros_like(rsend)
    for m in range(3):
        sums = jnp.sum(racc[m], axis=1, keepdims=True)
        rsend[m : m + 1, :] = jnp.sum(jnp.where(wide, sums, 0.0), axis=0, keepdims=True)
    r_copies = exchange(
        "col", c, NC, lambda peer: rsend, lambda d: rin.at[d - 1], r_ss, r_rs
    )
    mine = pl.ds(pl.multiple_of(me * 8, 8), 8)
    for copy in c_copies:
        copy.wait_recv()
    cfull[mine, :] = csend[mine, :] + jnp.sum(cin[...], axis=0)
    a_copies = exchange(
        "row", me, NR, lambda peer: cfull.at[mine, :], lambda d: cfull.at[mine, :], a_ss, a_rs
    )
    for copy in r_copies:
        copy.wait_recv()
    row_sum = rsend[...] + jnp.sum(rin[...], axis=0)
    row_new = 0.8 * row_old[...] + 0.2 * (row_sum[0:3] / FF + 1e-30)
    row_out[...] = row_new
    row_inv = 1.0 / row_new
    columns = [
        jnp.sum(jnp.where(wide, row_inv[m : m + 1], 0.0), axis=1, keepdims=True) for m in range(3)
    ]
    for copy in a_copies:
        copy.wait_recv()
    for m in range(3):
        for k in range(FL // 128):
            at = m * (FL // 128) + k
            cflat[m : m + 1, k * 128 : (k + 1) * 128] = cfull[at : at + 1, :]
    col_new = 0.8 * col_old[...] + 0.2 * (cflat[...] / D + 1e-30)
    col_out[...] = col_new
    cinv[...] = 1.0 / col_new
    racc[...] = jnp.zeros_like(racc)
    for m in range(3):
        @pl.loop(0, FL // 256)
        def _(i):
            lanes = sub(0, i)
            grad = big[m * DL : (m + 1) * DL, lanes]
            square = grad * grad * cinv[m : m + 1, lanes]
            racc[m] += square[:, 0:128] + square[:, 128:256]
        qsend[m : m + 1, :] = jnp.sum(racc[m] * columns[m], axis=0, keepdims=True)
    q_copies = exchange(
        "row", me, NR, lambda peer: qsend, lambda d: qin.at[d - 1], q_ss, q_rs
    )
    for copy in q_copies:
        copy.wait_recv()
    qmid[...] = qsend[...] + jnp.sum(qin[...], axis=0)
    l_copies = exchange(
        "col", c, NC, lambda peer: qmid, lambda d: qmid_in.at[d - 1], l_ss, l_rs
    )
    for copy in l_copies:
        copy.wait_recv()
    total_out[...] = qmid[...] + jnp.sum(qmid_in[...], axis=0)
    for copy in sq_copies + n_copies + d_copies + y_copies:
        copy.wait_send()
    for copy in c_copies + r_copies + a_copies + q_copies + l_copies:
        copy.wait_send()
    for one in drains:
        one.drain()
    for copy in (hidden_copy, normed_copy, dy_copy, grads_copy):
        copy.wait()


def whole(space=pltpu.VMEM):
    return pl.BlockSpec(memory_space=space)


def step(teacher, projection, student, gain, w_gate, w_up, w_down, row_old, col_old):
    sem = pltpu.SemaphoreType.DMA
    half = TILE // 2
    return pl.pallas_call(
        step_kernel,
        out_shape=(
            jax.ShapeDtypeStruct((TOKENS, DL), BF16),
            jax.ShapeDtypeStruct((TOKENS, DL), BF16),
            jax.ShapeDtypeStruct((TOKENS, FL), BF16),
            jax.ShapeDtypeStruct((TOKENS, 2 * FL), BF16),
            jax.ShapeDtypeStruct((3, DL), F32),
            jax.ShapeDtypeStruct((3, FL), F32),
            jax.ShapeDtypeStruct((8, 128), F32),
        ),
        in_specs=[
            whole(), whole(pl.ANY), whole(), whole(), whole(pl.ANY), whole(pl.ANY), whole(pl.ANY),
            whole(), whole(),
        ],
        out_specs=(whole(pl.ANY),) * 4 + (whole(),) * 3,
        scratch_shapes=[
            pltpu.VMEM(projection.shape, BF16),
            pltpu.VMEM((DL, FL), BF16),
            pltpu.VMEM((DL, FL), BF16),
            pltpu.VMEM((DL, FL), BF16),
            pltpu.VMEM((8, 128), F32),
            pltpu.VMEM((NR - 1, 8, 128), F32),
            pltpu.VMEM((NR, TL, DL), BF16),
            pltpu.VMEM((NR - 1, TL, DL), BF16),
            pltpu.VMEM((TOKENS, DL), BF16),
            pltpu.VMEM((TOKENS, 2 * FL), BF16),
            pltpu.VMEM((6, 64, 2 * TILE), BF16),
            pltpu.VMEM((6, 64, 2 * TILE), F32),
            pltpu.VMEM((6, 6, 64, TILE), BF16),
            pltpu.VMEM((6, 2, 64, TILE), BF16),
            pltpu.VMEM((6, 6, 16, TILE), BF16),
            pltpu.VMEM((6, 2, 16, TILE), BF16),
            pltpu.VMEM((TOKENS, FL), BF16),
            pltpu.VMEM((6, 16, TILE), F32),
            pltpu.VMEM((6, 16, TILE), F32),
            pltpu.VMEM((TOKENS, DL), F32),
            pltpu.VMEM((TOKENS, DL), BF16),
            pltpu.VMEM((NC - 1, TL, DL), BF16),
            pltpu.VMEM((TOKENS, DL), BF16),
            pltpu.VMEM((TOKENS, FL), BF16),
            pltpu.VMEM((6, 64, TILE), BF16),
            pltpu.VMEM((6, 64, TILE), F32),
            pltpu.VMEM((6, 6, 64, half), BF16),
            pltpu.VMEM((6, 2, 64, half), BF16),
            pltpu.VMEM((6, 6, 16, half), BF16),
            pltpu.VMEM((6, 2, 16, half), BF16),
            pltpu.VMEM((TOKENS, 2 * FL), BF16),
            pltpu.VMEM((3 * DL, FL), F32),
            pltpu.VMEM((2, DL, TOKENS), BF16),
            pltpu.VMEM((3, DL, 128), F32),
            pltpu.VMEM((128, 128), F32),
            pltpu.VMEM((NR - 1, 8, 128), F32),
            pltpu.VMEM((128, 128), F32),
            pltpu.VMEM((8, DL), F32),
            pltpu.VMEM((NC - 1, 8, DL), F32),
            pltpu.VMEM((3, FL), F32),
            pltpu.VMEM((3, FL), F32),
            pltpu.VMEM((8, 128), F32),
            pltpu.VMEM((NR - 1, 8, 128), F32),
            pltpu.VMEM((8, 128), F32),
            pltpu.VMEM((NC - 1, 8, 128), F32),
            sem((4,)), sem((4,)),
            sem((NR - 1,)), sem((NR - 1,)), sem((NR - 1,)), sem((NR - 1,)),
            sem((NC - 1,)), sem((NC - 1,)), sem((NC - 1,)), sem((NC - 1,)),
            sem((NC - 1,)), sem((NC - 1,)),
            sem((24, 6)), sem((24, 6)), sem((24, 4)), sem((24, 4)),
            sem((NR - 1,)), sem((NR - 1,)), sem((NR - 1,)), sem((NR - 1,)),
            sem((NC - 1,)), sem((NC - 1,)), sem((NR - 1,)), sem((NR - 1,)),
            sem((NC - 1,)), sem((NC - 1,)),
        ],
        compiler_params=pltpu.CompilerParams(
            collective_id=0, has_side_effects=True, vmem_limit_bytes=VMEM_LIMIT
        ),
        name="step",
    )(teacher, projection, student, gain, w_gate, w_up, w_down, row_old, col_old)


def update_kernel(normed, dy, hidden, gate_in, up_in, row_new, col_new, total, out0, out1, out2, left, scale):
    @pl.when(pl.program_id(0) == 0)
    def _():
        left[0] = normed[...].astype(F32).T.astype(BF16)
        left[1] = dy[...].astype(F32).T.astype(BF16)
        diag = eye(DL, DL)
        for m in range(3):
            mean = jnp.sum(total[m : m + 1, :], axis=1, keepdims=True) / (float(D) * FF)
            clip = 1.0 / jnp.maximum(1.0, jnp.sqrt(mean))
            column = jnp.sum(
                jnp.where(diag, row_new[m : m + 1, :], 0.0), axis=1, keepdims=True
            )
            scale[m] = jnp.broadcast_to(clip / jnp.sqrt(column), (DL, 128))

    for m, (lhs, rhs, out) in enumerate(
        ((left[0], gate_in, out0), (left[0], up_in, out1), (left[1], hidden, out2))
    ):
        grad = jnp.dot(lhs, rhs[...], preferred_element_type=F32)
        lane = 1.0 / jnp.sqrt(col_new[m : m + 1, :])
        for k in range(TILE // 128):
            at = slice(k * 128, (k + 1) * 128)
            out[:, at] = (grad[:, at] * scale[m] * lane[:, at]).astype(BF16)


def update(normed, dy, hidden, grads, row_new, col_new, total):
    full = lambda shape: pl.BlockSpec(shape, lambda i: (0, 0))
    tile = pl.BlockSpec((DL, TILE), lambda i: (0, i))
    return pl.pallas_call(
        update_kernel,
        grid=(FL // TILE,),
        out_shape=(jax.ShapeDtypeStruct((DL, FL), BF16),) * 3,
        in_specs=[
            full((TOKENS, DL)),
            full((TOKENS, DL)),
            pl.BlockSpec((TOKENS, TILE), lambda i: (0, i)),
            pl.BlockSpec((TOKENS, TILE), lambda i: (0, 2 * i)),
            pl.BlockSpec((TOKENS, TILE), lambda i: (0, 2 * i + 1)),
            full((3, DL)),
            pl.BlockSpec((3, TILE), lambda i: (0, i)),
            full((8, 128)),
        ],
        out_specs=(tile,) * 3,
        scratch_shapes=[pltpu.VMEM((2, DL, TOKENS), BF16), pltpu.VMEM((3, DL, 128), F32)],
        compiler_params=pltpu.CompilerParams(dimension_semantics=("arbitrary",)),
        name="update",
    )(normed, dy, hidden, grads, grads, row_new, col_new, total)


def shards(teacher_rows, projection, student_in, norm_gain, w_gate, w_up, w_down, row_old, col_old):
    normed, dy, hidden, grads, row_new, col_new, total = step(
        teacher_rows, projection, student_in, norm_gain[None, :], w_gate, w_up, w_down,
        row_old, col_old,
    )
    out = update(normed, dy, hidden, grads, row_new, col_new, total)
    return (*out, row_new, col_new, 0.5 * total[3, 0] / TOKENS)


def solution(mesh):
    placed = (
        P("col", "row"),
        P("row", None),
        P("col", "row"),
        P("row"),
        P("row", "col"),
        P("row", "col"),
        P("row", "col"),
        P(None, "row"),
        P(None, "col"),
    )
    return jax.shard_map(
        shards,
        mesh=mesh,
        in_specs=placed,
        out_specs=(
            P("row", "col"),
            P("row", "col"),
            P("row", "col"),
            P(None, "row"),
            P(None, "col"),
            P(),
        ),
        check_vma=False,
    )
```

time: 190 us -> 177 us (0.932)
  Pallas kernels: 184 us -> 170 us
    pallas_call x1 -> x0, Pallas kernels: 39.4 us -> none  [stats(): pl.pallas_call(stats_kernel, out_shape=(jax.ShapeDtypeStruct((3, DL), F32...]
    pallas_call x1, Pallas kernels: 135 us -> 162 us  [step(): pl.pallas_call(step_kernel, out_shape=(jax.ShapeDtypeStruct((TOKENS, DL),...]
where the time goes in v2:
time: 177 us
  Pallas kernels  170 us (96%)
  local copies, waits for them, and re-layouts  3.67 us (2%)
  between operations  2.45 us (1%)
    pallas_call x1, Pallas kernels, step(): pl.pallas_call(step_kernel, out_shape=(jax.ShapeDtypeStruct((TOKENS, DL),...  162 us
    pallas_call x1, Pallas kernels, update(): pl.pallas_call(update_kernel, grid=(FL // TILE,), out_shape=(jax.ShapeDty...  8.88 us

profile of v2, /device:TPU:1, one launch (start us, length us, event | category | flops | bytes accessed | tf_op | source)
XLA Modules:
  0.0 176.6 jit_solution(13808024097353985902)
XLA Ops:
  0.6 1.2 broadcast_in_dim.3.gain
  1.9 161.6 %step.1 = (bf16[256,288]{1,0:T(8,128)(2,1)}, bf16[256,288]{1,0:T(8,128)(2,1)}, bf16[256,4608]{1,0:T(8,128)(2,1)}, bf16[256,9216]{1,0:T(8,128)(2,1)}, f32[3,288]{...) custom-call(bf16[32,512]{1,0:T(8,128)(2,1)} %teacher.1, bf16[512,4608]{1,0:T(8,128)(2,1)} %projection.1, ...), custom_call_target="tpu_custom_call" | custom-call | tf_op jit(solution)/shard_map/step/pallas_call | solution.py:549
  163.5 0.0 copy-start.1
  163.5 0.0 copy-start
  163.5 8.9 %update.1 = (bf16[288,4608]{1,0:T(8,128)(2,1)}, bf16[288,4608]{1,0:T(8,128)(2,1)}, bf16[288,4608]{1,0:T(8,128)(2,1)}) custom-call(bf16[256,288]{1,0:T(8,128)(2,1)} %get-tuple-element.16.normed, bf16[256,288]{1,0:T(8,128)(2,1)} %get-tuple-element.17.dy, bf16[256,4608]{1,0:T(8,128)(2,1)} %get-tuple-element.18.hidden, ...), custom_call_target="tpu_custom_call" | custom-call | tf_op jit(solution)/shard_map/update/pallas_call | solution.py:654
  172.4 1.2 slice.3
  174.2 0.0 copy-done.1
  174.3 0.6 copy.17
  174.9 0.0 copy-done
  174.9 0.6 copy.18
Async XLA Ops:
  163.5 10.7 %copy-start.1 = (f32[3,288]{1,0:T(4,128)S(1)}, f32[3,288]{1,0:T(4,128)}, u32[]{:S(2)}) copy-start(f32[3,288]{1,0:T(4,128)} %get-tuple-element.35.row_new) | copy-start | bytes 10372
  163.5 11.3 %copy-start = (f32[3,4608]{1,0:T(4,128)S(1)}, f32[3,4608]{1,0:T(4,128)}, u32[]{:S(2)}) copy-start(f32[3,4608]{1,0:T(4,128)} %get-tuple-element.36.col_new) | copy-start | bytes 165892

commit v3 on v2

--- a/solution.py
+++ b/solution.py
@@ -173,14 +173,14 @@
 
 def step_kernel(
     teacher, projection, student, gain, w_gate, w_up, w_down, row_old, col_old,
-    normed_out, dy_out, hidden_out, grads_out, row_out, col_out, total_out,
+    out0, out1, out2, row_out, col_out, total_out,
     proj_v, wg_v, wu_v, wd_v, sq, sq_in, tpart, tpart_in, normed, part, mid, mid32, recv1, acc1,
     recv2, acc2, hidden, act_v, ups_v, down_acc, down_part, down_in, dy, gpart, gmid, gmid32,
     grecv1, gacc1, grecv2, gacc2, grads, big,
-    left, racc, csend, cin, cfull, rsend, rin, cflat, cinv, qsend, qin, qmid, qmid_in,
+    left, racc, pacc, csend, cin, cfull, rsend, rin, cnew, qsend, qin, kpart, kin, kfull,
     load_sem, out_sem, sq_ss, sq_rs, t_ss, t_rs, n_ss, n_rs, d_ss, d_rs, y_ss, y_rs,
     s_ss, s_rs, g_ss, g_rs,
-    c_ss, c_rs, a_ss, a_rs, r_ss, r_rs, q_ss, q_rs, l_ss, l_rs,
+    c_ss, c_rs, a_ss, a_rs, r_ss, r_rs, q_ss, q_rs, k_ss, k_rs, m_ss, m_rs,
 ):
     me = lax.axis_index("row")
     c = lax.axis_index("col")
@@ -201,10 +201,6 @@
     sq[...] = jnp.broadcast_to(
         jnp.sum(jnp.where(diag, sums, 0.0), axis=0, keepdims=True), (8, 128)
     )
-    met()
-    sq_copies = exchange(
-        "row", me, NR, lambda peer: sq, lambda d: sq_in.at[d - 1], sq_ss, sq_rs
-    )
     loads[0].wait()
     for i in range(4):
         product = jnp.dot(
@@ -212,6 +208,10 @@
         )
         for j in range(4):
             tpart[i * 4 + j] = product[:, j * DL : (j + 1) * DL].astype(BF16)
+    met()
+    sq_copies = exchange(
+        "row", me, NR, lambda peer: sq, lambda d: sq_in.at[d - 1], sq_ss, sq_rs
+    )
     t_copies = exchange(
         "row", me, NR, lambda peer: tpart.at[peer], lambda d: tpart_in.at[d - 1], t_ss, t_rs
     )
@@ -220,7 +220,7 @@
     total = sq[0:1] + jnp.sum(sq_in[:, 0, :], axis=0, keepdims=True)
     mean_sq = jnp.sum(jnp.where(diag, total, 0.0), axis=1, keepdims=True) / D
     inv_rms = 1.0 / jnp.sqrt(mean_sq + 1e-06)
-    normed[own, :] = (inputs * inv_rms * gain[...].astype(F32)).astype(BF16)
+    normed[own, :] = (inputs * inv_rms * gain[...].astype(F32).reshape(1, DL)).astype(BF16)
     n_copies = exchange(
         "col", c, NC, lambda peer: normed.at[own, :], lambda d: normed.at[own, :], n_ss, n_rs
     )
@@ -239,30 +239,26 @@
         base = pl.multiple_of(first[s][0] * 64, 64)
         return base, pl.ds(pl.multiple_of(base + second[s][0] * 16, 16), 16)
 
-    def sub(lo, i):
-        return pl.ds(pl.multiple_of(lo + i * 256, 128), 256)
+    def tile(k):
+        return slice(k * TILE, (k + 1) * TILE)
 
     def run(stages):
-        for t in range(len(stages) + 2):
-            order = [j for j in range(3) if t == j] + [
-                j for j in range(3) if 0 < t - j < len(stages)
-            ]
-            for j in order:
+        for stage in stages:
+            for j in range(3):
                 for s in range(2):
-                    stages[t - j](s, j)
+                    stage(s, j)
 
     sc1, sc2, ga1, ga2 = {}, {}, {}, {}
 
     def f_start(s, j):
         k = 3 * s + j
 
-        @pl.loop(0, 3)
-        def _(i):
-            rows = normed[...]
-            for weights, off in ((wg_v, 0), (wu_v, TILE)):
-                value = jnp.dot(rows, weights[:, sub(k * TILE, i)], preferred_element_type=F32)
-                big[s * TOKENS : (s + 1) * TOKENS, sub(j * 2 * TILE + off, i)] = value
-                part[:, sub(k * 2 * TILE + off, i)] = value.astype(BF16)
+        for weights, off in ((wg_v, 0), (wu_v, TILE)):
+            value = jnp.dot(normed[...], weights[:, tile(k)], preferred_element_type=F32)
+            lo = j * 2 * TILE + off
+            big[s * TOKENS : (s + 1) * TOKENS, lo : lo + TILE] = value
+            lo = k * 2 * TILE + off
+            part[:, lo : lo + TILE] = value.astype(BF16)
 
         sc1[k] = Scatter(
             part, big.at[s * TOKENS : (s + 1) * TOKENS], 64, k * 2 * TILE, j * 2 * TILE, 2 * TILE,
@@ -270,6 +266,33 @@
         )
         sc1[k].start()
         drains.append(sc1[k])
+
+    gram = {}
+
+    def f_gram(s, j):
+        if s == 0 and j == 0:
+            kpart[...] = lax.dot_general(
+                normed[...], normed[...], (((1,), (1,)), ((), ())), preferred_element_type=F32
+            ).astype(BF16)
+            gram["sum"] = exchange(
+                "row", me, NR,
+                lambda peer: kpart.at[pl.ds(pl.multiple_of(peer * 16, 16), 16), :],
+                lambda d: kin.at[d - 1], k_ss, k_rs,
+            )
+
+    def f_gram_all(s, j):
+        if s == 0 and j == 0:
+            rows = pl.ds(pl.multiple_of(me * 16, 16), 16)
+            for copy in gram["sum"]:
+                copy.wait_recv()
+            value = kpart[rows, :].astype(F32)
+            for d in range(NR - 1):
+                value = value + kin[d].astype(F32)
+            kfull[rows, :] = value.astype(BF16)
+            gram["all"] = exchange(
+                "row", me, NR, lambda peer: kfull.at[rows, :], lambda d: kfull.at[rows, :],
+                m_ss, m_rs,
+            )
 
     def f_relay1(s, j):
         sc1[3 * s + j].relay()
@@ -323,15 +346,12 @@
         k = 3 * s + j
         ga2[k].done()
 
-        @pl.loop(0, 3)
-        def _(i):
-            lanes = sub(k * TILE, i)
-            down_acc[...] += lax.dot_general(
-                hidden[:, lanes], wd_v[:, lanes], (((1,), (1,)), ((), ())),
-                preferred_element_type=F32,
-            )
-
-    run((f_start, f_relay1, f_second, f_relay2, f_hidden, f_relay3, f_gather, f_relay4, f_down))
+        down_acc[...] += lax.dot_general(
+            hidden[:, tile(k)], wd_v[:, tile(k)], (((1,), (1,)), ((), ())),
+            preferred_element_type=F32,
+        )
+
+    run((f_start, f_gram, f_relay1, f_second, f_gram_all, f_relay2, f_hidden, f_relay3, f_gather, f_relay4, f_down))
 
     down_part[...] = down_acc[...].astype(BF16)
     d_copies = exchange(
@@ -339,10 +359,6 @@
         lambda peer: down_part.at[pl.ds(pl.multiple_of(peer * TL, TL), TL), :],
         lambda d: down_in.at[d - 1], d_ss, d_rs,
     )
-    hidden_copy = pltpu.make_async_copy(hidden, hidden_out, out_sem.at[0])
-    hidden_copy.start()
-    normed_copy = pltpu.make_async_copy(normed, normed_out, out_sem.at[1])
-    normed_copy.start()
     finish(t_copies)
     target = tpart[me].astype(F32)
     for d in range(NR - 1):
@@ -358,27 +374,23 @@
     y_copies = exchange(
         "col", c, NC, lambda peer: dy.at[own, :], lambda d: dy.at[own, :], y_ss, y_rs
     )
-    qsend[...] = jnp.zeros_like(qsend) + jnp.sum(residue * residue)
+    rsend[...] = jnp.zeros_like(rsend) + jnp.sum(residue * residue)
     left[0] = normed[...].astype(F32).T.astype(BF16)
     for copy in y_copies:
         copy.wait_recv()
-    dy_copy = pltpu.make_async_copy(dy, dy_out, out_sem.at[2])
-    dy_copy.start()
 
     gs1, gs2, gg1, gg2 = {}, {}, {}, {}
     half = TILE // 2
     csend[...] = jnp.zeros_like(csend)
     racc[...] = jnp.zeros_like(racc)
+    pacc[...] = jnp.zeros_like(pacc)
 
     def b_start(s, j):
         k = 3 * s + j
 
-        @pl.loop(0, 3)
-        def _(i):
-            lanes = sub(k * TILE, i)
-            value = jnp.dot(dy[...], wd_v[:, lanes], preferred_element_type=F32)
-            big[0:TOKENS, lanes] = value
-            gpart[:, lanes] = value.astype(BF16)
+        value = jnp.dot(dy[...], wd_v[:, tile(k)], preferred_element_type=F32)
+        big[0:TOKENS, tile(k)] = value
+        gpart[:, tile(k)] = value.astype(BF16)
 
         gs1[k] = Scatter(
             gpart, big.at[0:TOKENS], 64, k * TILE, k * TILE, TILE, *first[s],
@@ -436,106 +448,142 @@
     def b_relay4(s, j):
         gg2[3 * s + j].relay()
 
-    def sums_of(m, k, rhs, lo):
-        @pl.loop(0, 3)
-        def _(i):
-            grad = jnp.dot(left[m // 2], rhs[:, sub(lo, i)], preferred_element_type=F32)
-            big[m * DL : (m + 1) * DL, sub(k * TILE, i)] = grad
-            square = grad * grad
-            racc[m] += square[:, 0:128] + square[:, 128:256]
-            column = jnp.sum(square, axis=0, keepdims=True)
-            for n in range(2):
-                csend[pl.ds(m * (FL // 128) + k * 6 + i * 2 + n, 1), :] = column[
-                    :, n * 128 : (n + 1) * 128
-                ]
-
-    def b_sums(s, j):
-        k = 3 * s + j
-        gg2[k].done()
-        sums_of(0, k, grads, 2 * k * TILE)
-        sums_of(1, k, grads, (2 * k + 1) * TILE)
+    def weigh(m, k, grad):
+        square = grad * grad
+        folded = square[:, 0:128]
+        for n in range(1, TILE // 128):
+            folded = folded + square[:, n * 128 : (n + 1) * 128]
+        racc[m] += folded
+        return square
+
+    def weighted(m, k, square):
+        lanes = slice(k * TILE, (k + 1) * TILE)
+        square = square * (1.0 / cnew[m : m + 1, lanes])
+        folded = square[:, 0:128]
+        for n in range(1, TILE // 128):
+            folded = folded + square[:, n * 128 : (n + 1) * 128]
+        pacc[m] += folded
 
     def b_relay1_and_down(s, j):
-        if s == 0 and j == 0:
+        k = 3 * s + j
+        if k == 0:
             left[1] = dy[...].astype(F32).T.astype(BF16)
         b_relay1(s, j)
-        sums_of(2, 3 * s + j, hidden, (3 * s + j) * TILE)
+        grad = jnp.dot(left[1], hidden[:, tile(k)], preferred_element_type=F32)
+        big[2 * DL : 3 * DL, tile(k)] = grad
+        column = jnp.sum(weigh(2, k, grad), axis=0, keepdims=True)
+        for n in range(6):
+            at = k * 6 + n
+            csend[at : at + 1, :] = column[:, n * 128 : (n + 1) * 128]
+
+    cols = {}
+    mine = pl.ds(pl.multiple_of(me * 8, 8), 8)
+
+    def b_columns(s, j):
+        if s == 0 and j == 0:
+            cols["sum"] = exchange(
+                "row", me, NR,
+                lambda peer: csend.at[pl.ds(pl.multiple_of(peer * 8, 8), 8), :],
+                lambda d: cin.at[d - 1], c_ss, c_rs,
+            )
+
+    def b_columns_all(s, j):
+        if s == 0 and j == 0:
+            for copy in cols["sum"]:
+                copy.wait_recv()
+            cfull[mine, :] = csend[mine, :] + jnp.sum(cin[...], axis=0)
+            cols["all"] = exchange(
+                "row", me, NR, lambda peer: cfull.at[mine, :], lambda d: cfull.at[mine, :],
+                a_ss, a_rs,
+            )
+
+    def b_columns_use(s, j):
+        if s == 0 and j == 0:
+            for copy in cols["all"]:
+                copy.wait_recv()
+            for n in range(FL // 128):
+                cnew[2:3, n * 128 : (n + 1) * 128] = cfull[n : n + 1, :]
+            cnew[2:3, :] = 0.8 * col_old[2:3, :] + 0.2 * (cnew[2:3, :] / D + 1e-30)
+            for copy in gram["all"]:
+                copy.wait_recv()
+        k = 3 * s + j
+        grad = big[2 * DL : 3 * DL, tile(k)]
+        weighted(2, k, grad * grad)
+
+    def b_sums(s, j):
+        k = 3 * s + j
+        gg2[k].done()
+        for m in range(2):
+            at = slice((2 * k + m) * TILE, (2 * k + m + 1) * TILE)
+            rhs = grads[:, at]
+            spread = jnp.dot(kfull[...], rhs, preferred_element_type=F32)
+            column = jnp.sum(spread * rhs.astype(F32), axis=0, keepdims=True)
+            column = jnp.maximum(column, 0.0)
+            cnew[m : m + 1, tile(k)] = 0.8 * col_old[m : m + 1, tile(k)] + 0.2 * (
+                column / D + 1e-30
+            )
+            grad = jnp.dot(left[0], rhs, preferred_element_type=F32)
+            big[m * DL : (m + 1) * DL, tile(k)] = grad
+            weighted(m, k, weigh(m, k, grad))
 
     run(
         (
-            b_start, b_relay1_and_down, b_second, b_relay2, b_inputs, b_relay3, b_gather,
-            b_relay4, b_sums,
-        )
-    )
-    grads_copy = pltpu.make_async_copy(grads, grads_out, out_sem.at[3])
-    grads_copy.start()
-
-    c_copies = exchange(
-        "row", me, NR,
-        lambda peer: csend.at[pl.ds(pl.multiple_of(peer * 8, 8), 8), :],
-        lambda d: cin.at[d - 1], c_ss, c_rs,
+            b_start, b_relay1_and_down, b_columns, b_second, b_relay2, b_columns_all, b_inputs,
+            b_relay3, b_gather, b_columns_use, b_relay4, b_sums,
+        )
     )
     wide = eye(DL, DL)
-    rsend[...] = jnp.zeros_like(rsend)
     for m in range(3):
-        sums = jnp.sum(racc[m], axis=1, keepdims=True)
-        rsend[m : m + 1, :] = jnp.sum(jnp.where(wide, sums, 0.0), axis=0, keepdims=True)
+        for row, acc in ((m, racc), (3 + m, pacc)):
+            sums = jnp.sum(acc[m], axis=1, keepdims=True)
+            rsend[row : row + 1, :] = jnp.sum(
+                jnp.where(wide, sums, 0.0), axis=0, keepdims=True
+            )
     r_copies = exchange(
         "col", c, NC, lambda peer: rsend, lambda d: rin.at[d - 1], r_ss, r_rs
     )
-    mine = pl.ds(pl.multiple_of(me * 8, 8), 8)
-    for copy in c_copies:
-        copy.wait_recv()
-    cfull[mine, :] = csend[mine, :] + jnp.sum(cin[...], axis=0)
-    a_copies = exchange(
-        "row", me, NR, lambda peer: cfull.at[mine, :], lambda d: cfull.at[mine, :], a_ss, a_rs
-    )
+    col_out[...] = cnew[...]
+    cnew[...] = 1.0 / jnp.sqrt(cnew[...])
     for copy in r_copies:
         copy.wait_recv()
     row_sum = rsend[...] + jnp.sum(rin[...], axis=0)
     row_new = 0.8 * row_old[...] + 0.2 * (row_sum[0:3] / FF + 1e-30)
     row_out[...] = row_new
-    row_inv = 1.0 / row_new
-    columns = [
-        jnp.sum(jnp.where(wide, row_inv[m : m + 1], 0.0), axis=1, keepdims=True) for m in range(3)
-    ]
-    for copy in a_copies:
-        copy.wait_recv()
-    for m in range(3):
-        for k in range(FL // 128):
-            at = m * (FL // 128) + k
-            cflat[m : m + 1, k * 128 : (k + 1) * 128] = cfull[at : at + 1, :]
-    col_new = 0.8 * col_old[...] + 0.2 * (cflat[...] / D + 1e-30)
-    col_out[...] = col_new
-    cinv[...] = 1.0 / col_new
-    racc[...] = jnp.zeros_like(racc)
-    for m in range(3):
+    qsend[0:3, :] = jnp.broadcast_to(
+        jnp.sum(row_sum[3:6] / row_new, axis=1, keepdims=True), (3, 128)
+    )
+    qsend[3:8, :] = jnp.broadcast_to(row_sum[6:7, 0:1], (5, 128))
+    q_copies = exchange(
+        "row", me, NR, lambda peer: qsend, lambda d: qin.at[d - 1], q_ss, q_rs
+    )
+    scale = 1.0 / jnp.sqrt(row_new)
+    out_copies = []
+    for m, (staged, out) in enumerate(((wg_v, out0), (wu_v, out1), (wd_v, out2))):
+        racc[m] = jnp.broadcast_to(
+            jnp.sum(jnp.where(wide, scale[m : m + 1], 0.0), axis=1, keepdims=True), (DL, 128)
+        )
+
         @pl.loop(0, FL // 256)
         def _(i):
-            lanes = sub(0, i)
-            grad = big[m * DL : (m + 1) * DL, lanes]
-            square = grad * grad * cinv[m : m + 1, lanes]
-            racc[m] += square[:, 0:128] + square[:, 128:256]
-        qsend[m : m + 1, :] = jnp.sum(racc[m] * columns[m], axis=0, keepdims=True)
-    q_copies = exchange(
-        "row", me, NR, lambda peer: qsend, lambda d: qin.at[d - 1], q_ss, q_rs
-    )
+            for n in range(2):
+                lanes = pl.ds(pl.multiple_of(i * 256 + n * 128, 128), 128)
+                staged[:, lanes] = (
+                    big[m * DL : (m + 1) * DL, lanes] * racc[m] * cnew[m : m + 1, lanes]
+                ).astype(BF16)
+
+        copy = pltpu.make_async_copy(staged, out, out_sem.at[m])
+        copy.start()
+        out_copies.append(copy)
     for copy in q_copies:
         copy.wait_recv()
-    qmid[...] = qsend[...] + jnp.sum(qin[...], axis=0)
-    l_copies = exchange(
-        "col", c, NC, lambda peer: qmid, lambda d: qmid_in.at[d - 1], l_ss, l_rs
-    )
-    for copy in l_copies:
-        copy.wait_recv()
-    total_out[...] = qmid[...] + jnp.sum(qmid_in[...], axis=0)
-    for copy in sq_copies + n_copies + d_copies + y_copies:
+    total_out[...] = qsend[...] + jnp.sum(qin[...], axis=0)
+    for copy in sq_copies + n_copies + d_copies + y_copies + gram["sum"] + gram["all"]:
         copy.wait_send()
-    for copy in c_copies + r_copies + a_copies + q_copies + l_copies:
+    for copy in cols["sum"] + cols["all"] + r_copies + q_copies:
         copy.wait_send()
     for one in drains:
         one.drain()
-    for copy in (hidden_copy, normed_copy, dy_copy, grads_copy):
+    for copy in out_copies:
         copy.wait()
 
 
@@ -549,10 +597,9 @@
     return pl.pallas_call(
         step_kernel,
         out_shape=(
-            jax.ShapeDtypeStruct((TOKENS, DL), BF16),
-            jax.ShapeDtypeStruct((TOKENS, DL), BF16),
-            jax.ShapeDtypeStruct((TOKENS, FL), BF16),
-            jax.ShapeDtypeStruct((TOKENS, 2 * FL), BF16),
+            jax.ShapeDtypeStruct((DL, FL), BF16),
+            jax.ShapeDtypeStruct((DL, FL), BF16),
+            jax.ShapeDtypeStruct((DL, FL), BF16),
             jax.ShapeDtypeStruct((3, DL), F32),
             jax.ShapeDtypeStruct((3, FL), F32),
             jax.ShapeDtypeStruct((8, 128), F32),
@@ -561,7 +608,7 @@
             whole(), whole(pl.ANY), whole(), whole(), whole(pl.ANY), whole(pl.ANY), whole(pl.ANY),
             whole(), whole(),
         ],
-        out_specs=(whole(pl.ANY),) * 4 + (whole(),) * 3,
+        out_specs=(whole(pl.ANY),) * 3 + (whole(),) * 3,
         scratch_shapes=[
             pltpu.VMEM(projection.shape, BF16),
             pltpu.VMEM((DL, FL), BF16),
@@ -597,17 +644,18 @@
             pltpu.VMEM((3 * DL, FL), F32),
             pltpu.VMEM((2, DL, TOKENS), BF16),
             pltpu.VMEM((3, DL, 128), F32),
+            pltpu.VMEM((3, DL, 128), F32),
             pltpu.VMEM((128, 128), F32),
             pltpu.VMEM((NR - 1, 8, 128), F32),
             pltpu.VMEM((128, 128), F32),
             pltpu.VMEM((8, DL), F32),
             pltpu.VMEM((NC - 1, 8, DL), F32),
             pltpu.VMEM((3, FL), F32),
-            pltpu.VMEM((3, FL), F32),
             pltpu.VMEM((8, 128), F32),
             pltpu.VMEM((NR - 1, 8, 128), F32),
-            pltpu.VMEM((8, 128), F32),
-            pltpu.VMEM((NC - 1, 8, 128), F32),
+            pltpu.VMEM((TOKENS, TOKENS), BF16),
+            pltpu.VMEM((NR - 1, 16, TOKENS), BF16),
+            pltpu.VMEM((TOKENS, TOKENS), BF16),
             sem((4,)), sem((4,)),
             sem((NR - 1,)), sem((NR - 1,)), sem((NR - 1,)), sem((NR - 1,)),
             sem((NC - 1,)), sem((NC - 1,)), sem((NC - 1,)), sem((NC - 1,)),
@@ -615,7 +663,7 @@
             sem((24, 6)), sem((24, 6)), sem((24, 4)), sem((24, 4)),
             sem((NR - 1,)), sem((NR - 1,)), sem((NR - 1,)), sem((NR - 1,)),
             sem((NC - 1,)), sem((NC - 1,)), sem((NR - 1,)), sem((NR - 1,)),
-            sem((NC - 1,)), sem((NC - 1,)),
+            sem((NR - 1,)), sem((NR - 1,)), sem((NR - 1,)), sem((NR - 1,)),
         ],
         compiler_params=pltpu.CompilerParams(
             collective_id=0, has_side_effects=True, vmem_limit_bytes=VMEM_LIMIT
@@ -624,60 +672,34 @@
     )(teacher, projection, student, gain, w_gate, w_up, w_down, row_old, col_old)
 
 
-def update_kernel(normed, dy, hidden, gate_in, up_in, row_new, col_new, total, out0, out1, out2, left, scale):
-    @pl.when(pl.program_id(0) == 0)
-    def _():
-        left[0] = normed[...].astype(F32).T.astype(BF16)
-        left[1] = dy[...].astype(F32).T.astype(BF16)
-        diag = eye(DL, DL)
-        for m in range(3):
-            mean = jnp.sum(total[m : m + 1, :], axis=1, keepdims=True) / (float(D) * FF)
-            clip = 1.0 / jnp.maximum(1.0, jnp.sqrt(mean))
-            column = jnp.sum(
-                jnp.where(diag, row_new[m : m + 1, :], 0.0), axis=1, keepdims=True
-            )
-            scale[m] = jnp.broadcast_to(clip / jnp.sqrt(column), (DL, 128))
-
-    for m, (lhs, rhs, out) in enumerate(
-        ((left[0], gate_in, out0), (left[0], up_in, out1), (left[1], hidden, out2))
-    ):
-        grad = jnp.dot(lhs, rhs[...], preferred_element_type=F32)
-        lane = 1.0 / jnp.sqrt(col_new[m : m + 1, :])
+def clip_kernel(total, in0, in1, in2, out0, out1, out2):
+    for m, (value, out) in enumerate(((in0, out0), (in1, out1), (in2, out2))):
+        mean = total[m : m + 1, :] / (float(D) * FF)
+        clip = 1.0 / jnp.maximum(1.0, jnp.sqrt(mean))
         for k in range(TILE // 128):
             at = slice(k * 128, (k + 1) * 128)
-            out[:, at] = (grad[:, at] * scale[m] * lane[:, at]).astype(BF16)
-
-
-def update(normed, dy, hidden, grads, row_new, col_new, total):
-    full = lambda shape: pl.BlockSpec(shape, lambda i: (0, 0))
+            out[:, at] = (value[:, at].astype(F32) * clip).astype(BF16)
+
+
+def clipped(total, values):
     tile = pl.BlockSpec((DL, TILE), lambda i: (0, i))
     return pl.pallas_call(
-        update_kernel,
+        clip_kernel,
         grid=(FL // TILE,),
         out_shape=(jax.ShapeDtypeStruct((DL, FL), BF16),) * 3,
-        in_specs=[
-            full((TOKENS, DL)),
-            full((TOKENS, DL)),
-            pl.BlockSpec((TOKENS, TILE), lambda i: (0, i)),
-            pl.BlockSpec((TOKENS, TILE), lambda i: (0, 2 * i)),
-            pl.BlockSpec((TOKENS, TILE), lambda i: (0, 2 * i + 1)),
-            full((3, DL)),
-            pl.BlockSpec((3, TILE), lambda i: (0, i)),
-            full((8, 128)),
-        ],
+        in_specs=[pl.BlockSpec((8, 128), lambda i: (0, 0)), tile, tile, tile],
         out_specs=(tile,) * 3,
-        scratch_shapes=[pltpu.VMEM((2, DL, TOKENS), BF16), pltpu.VMEM((3, DL, 128), F32)],
         compiler_params=pltpu.CompilerParams(dimension_semantics=("arbitrary",)),
-        name="update",
-    )(normed, dy, hidden, grads, grads, row_new, col_new, total)
+        name="clip",
+    )(total, *values)
 
 
 def shards(teacher_rows, projection, student_in, norm_gain, w_gate, w_up, w_down, row_old, col_old):
-    normed, dy, hidden, grads, row_new, col_new, total = step(
-        teacher_rows, projection, student_in, norm_gain[None, :], w_gate, w_up, w_down,
+    *values, row_new, col_new, total = step(
+        teacher_rows, projection, student_in, norm_gain, w_gate, w_up, w_down,
         row_old, col_old,
     )
-    out = update(normed, dy, hidden, grads, row_new, col_new, total)
+    out = clipped(total, values)
     return (*out, row_new, col_new, 0.5 * total[3, 0] / TOKENS)
 
 

time: 177 us -> 154 us (0.87)
  Pallas kernels: 170 us -> 149 us
    pallas_call x2, Pallas kernels: 170 us -> 149 us  [the longest x1 141 us: step(): pl.pallas_call(step_kernel, out_shape=(jax.ShapeDtypeStruct((DL, FL), BF1...]
where the time goes in v3:
time: 154 us; the launch traced here: 153 us
  Pallas kernels  149 us (97%)
  between operations  2.45 us (2%)
  local copies, waits for them, and re-layouts  2.42 us (2%)
    pallas_call x1, Pallas kernels, step(): pl.pallas_call(step_kernel, out_shape=(jax.ShapeDtypeStruct((DL, FL), BF1...  141 us
    pallas_call x1, Pallas kernels, clipped(): pl.pallas_call(clip_kernel, grid=(FL // TILE,), out_shape=(jax.ShapeDtype...  7.74 us

profile of v3, /device:TPU:1, one launch (start us, length us, event | category | flops | bytes accessed | tf_op | source)
XLA Modules:
  0.0 153.4 jit_solution(9003794625321707456)
XLA Ops:
  0.6 140.8 %step.1 = (bf16[288,4608]{1,0:T(8,128)(2,1)}, bf16[288,4608]{1,0:T(8,128)(2,1)}, bf16[288,4608]{1,0:T(8,128)(2,1)}, f32[3,288]{1,0:T(4,128)}, f32[3,4608]{1,0:T(4,128)}, /*index=5*/f32[8,128]{1,0:T(8,128)}) custom-call(bf16[32,512]{1,0:T(8,128)(2,1)} %teacher.1, bf16[512,4608]{1,0:T(8,128)(2,1)} %projection.1, bf16[32,288]{1,0:T(8,128)(2,1)} %student.1, ...), custom_call_target="tpu_custom_call" | custom-call | tf_op jit(solution)/shard_map/step/pallas_call | solution.py:597
  141.4 0.0 copy-start.1
  141.4 0.0 copy-start
  141.4 7.7 %clip.1 = (bf16[288,4608]{1,0:T(8,128)(2,1)}, bf16[288,4608]{1,0:T(8,128)(2,1)}, bf16[288,4608]{1,0:T(8,128)(2,1)}) custom-call(f32[8,128]{1,0:T(8,128)} %get-tuple-element.15.total, bf16[288,4608]{1,0:T(8,128)(2,1)} %get-tuple-element.16.in0, bf16[288,4608]{1,0:T(8,128)(2,1)} %get-tuple-element.17.in1, bf16[288,4608]{1,0:T(8,128)(2,1)} %get-tuple-element.18.in2), custom_call_target="tpu_custom_call" | custom-call | tf_op jit(solution)/shard_map/clip/pallas_call | solution.py:686
  149.2 1.2 slice.3
  151.0 0.0 copy-done.1
  151.0 0.6 copy.17
  151.6 0.0 copy-done
  151.6 0.6 copy.18
Async XLA Ops:
  141.4 9.6 %copy-start.1 = (f32[3,288]{1,0:T(4,128)S(1)}, f32[3,288]{1,0:T(4,128)}, u32[]{:S(2)}) copy-start(f32[3,288]{1,0:T(4,128)} %get-tuple-element.33) | copy-start | bytes 10372
  141.4 10.2 %copy-start = (f32[3,4608]{1,0:T(4,128)S(1)}, f32[3,4608]{1,0:T(4,128)}, u32[]{:S(2)}) copy-start(f32[3,4608]{1,0:T(4,128)} %get-tuple-element.34) | copy-start | bytes 165892
